TPU v7x, 768 devices: a whole 4x8x12 slice. The times are simulated.
768 devices in a mesh: dp: 48 (over z_lo, x, core), tensor: 16 (over z_hi, y).
Axes of the slice: x: 4, y: 8, z: 12 (z_hi: 2, z_lo: 6; z = z_hi * 6 + z_lo), core: 2. Of those that a mesh axis runs over, the one named last changes fastest.
Arguments:
- tokens: bfloat16 [24576, 8192], P('dp'), may hold values from -40 to 40
- cotangent: bfloat16 [24576, 2048], P('dp', 'tensor'), may hold values from -260 to 260
- master: float32 [8208, 2048], P('dp', 'tensor'), may hold values from -0.0625 to 0.0625
- first_moment: float32 [8208, 2048], P('dp', 'tensor'), may hold values from -0.0014648438 to 0.0014648438
- second_moment: float32 [8208, 2048], P('dp', 'tensor'), may hold values from 1.7881393e-09 to 1.7881393e-07
- old_rows: int32 [8208], P('dp'), may hold values from 0 to 8207, as said below
Outputs:
- keys_values: bfloat16 [24576, 2048], P('dp', 'tensor')
- update: float32 [8208, 2048], P('dp', 'tensor')
Inputs may be any that keep to these rules, and one draw needn't show every extreme that they name: `old_rows`: every row 0 to 8207 is named by exactly one slot. Rows j * 171 to (j + 1) * 171 - 1 belong to new owner j; the slots of one device name at most 8 rows of one owner.
All inputs are finite; a program needn't handle non-finite values.
Results may differ from a plain program's by a relative error of at most 0.0049.
Values may be sent and summed in bfloat16 or wider, within the bound.
No kernel may reach another device: no remote copies, remote signals or barrier semaphores. Data moves between devices by JAX's collectives and lax.ppermute only.
A program may use at most 64 MiB of HBM per device.

v0:
```python
import functools

import jax
import jax.numpy as jnp
from jax import lax
from jax.experimental import pallas as pl
from jax.experimental.pallas import tpu as pltpu
from jax.sharding import PartitionSpec as P

beta_one = 0.9
beta_two = 0.95
adam_eps = 1e-08
clip_norm = 1.0

F32, BF16 = jnp.float32, jnp.bfloat16
NZ, NX, NC = 6, 4, 2
DP = NZ * NX * NC
CAP = 8
PAD = 176
BLOCKS = 8


FIRST, SECOND = (1, 3), (3, 1)


def shift(value, dx=(0, 0), dc=0):
    pairs = []
    for z in range(NZ):
        for x in range(NX):
            for c in range(NC):
                source = (z * NX + x) * NC + c
                pairs.append((source, (z * NX + (x ^ dx[c])) * NC + (c ^ dc)))
    return lax.ppermute(value, "dp", pairs)


def along_z(value):
    rest = NX * NC
    groups = [[z * rest + i for z in range(NZ)] for i in range(rest)]
    return lax.all_to_all(
        value, "dp", split_axis=0, concat_axis=0, tiled=True, axis_index_groups=groups
    )


def iota(shape, axis):
    return lax.broadcasted_iota(jnp.int32, shape, axis).astype(F32)


def route_kernel(rows_ref, master_ref, first_ref, second_ref, out_ref):
    count = rows_ref.shape[1]
    rows_dev = float(count)
    along = rows_ref[...].astype(F32)
    line, column = iota((count, count), 0), iota((count, count), 1)
    down = jnp.sum(jnp.where(line == column, along, 0.0), axis=1, keepdims=True)
    owner_down = jnp.sum(
        jnp.where(down >= rows_dev * (iota((count, 128), 1) + 1.0), 1.0, 0.0), axis=1, keepdims=True
    )
    owner_along = jnp.sum(
        jnp.where(along >= rows_dev * (iota((DP, count), 0) + 1.0), 1.0, 0.0), axis=0, keepdims=True
    )
    before = jnp.where((owner_down == owner_along) & (line < column), 1.0, 0.0)
    within = jnp.sum(before, axis=0, keepdims=True)
    code = owner_along * CAP + within
    pick = jnp.where(code == iota((DP * CAP, count), 0), 1.0, 0.0).astype(BF16)
    label = jnp.broadcast_to(down - rows_dev * owner_down + 1.0, (count, 128))
    data = jnp.concatenate(
        [master_ref[...], first_ref[...], second_ref[...], label], axis=1
    ).astype(BF16)
    sent = jnp.dot(pick, data, preferred_element_type=F32)
    parts = [sent[:, 128 * k : 128 * k + 128].reshape(DP, CAP, 128) for k in range(4)]
    out_ref[...] = jnp.concatenate(parts, axis=1).astype(BF16)


def route(rows, master, first, second):
    return pl.pallas_call(
        route_kernel,
        out_shape=jax.ShapeDtypeStruct((DP, 4 * CAP, 128), BF16),
        name="route",
    )(rows.reshape(1, -1), master, first, second)


def place_kernel(box_ref, weight_ref, first_ref, second_ref):
    box = box_ref[...].astype(F32)
    parts = [box[:, CAP * k : CAP * k + CAP, :].reshape(DP * CAP, 128) for k in range(4)]
    label = parts[3]
    lane = iota((DP * CAP, 128), 1)
    pick = jnp.concatenate(
        [jnp.where(label == lane + 1.0, 1.0, 0.0), jnp.where(label == lane + 129.0, 1.0, 0.0)],
        axis=1,
    ).astype(BF16)
    data = jnp.concatenate(parts[:3], axis=1).astype(BF16)
    placed = lax.dot_general(
        pick, data, (((0,), (0,)), ((), ())), preferred_element_type=F32
    )
    weight_ref[...] = placed[:PAD, :128].astype(BF16)
    first_ref[...] = placed[:PAD, 128:256]
    second_ref[...] = placed[:PAD, 256:384]


def place(box):
    return pl.pallas_call(
        place_kernel,
        out_shape=(
            jax.ShapeDtypeStruct((PAD, 128), BF16),
            jax.ShapeDtypeStruct((PAD, 128), F32),
            jax.ShapeDtypeStruct((PAD, 128), F32),
        ),
        name="place",
    )(box)


def pick_of(key, values):
    chosen = jnp.int32(values[-1])
    for index, value in enumerate(values[:-1]):
        chosen = jnp.where(key == index, jnp.int32(value), chosen)
    return chosen


def fetch(tokens_hbm, tokens_ref, sems):
    width = tokens_ref.shape[1] // BLOCKS
    copies = [
        pltpu.make_async_copy(
            tokens_hbm.at[:, pl.ds(i * width, width)],
            tokens_ref.at[:, pl.ds(i * width, width)],
            sems.at[i],
        )
        for i in range(BLOCKS)
    ]
    for copy in copies:
        copy.start()
    return copies


def grad_kernel(
    rows_dev, me_ref, cot_ref, tokens_hbm, send_ref, keep_ref, tokens_ref, whole_ref, sems
):
    features = tokens_ref.shape[1]
    width = features // BLOCKS
    copies = fetch(tokens_hbm, tokens_ref, sems)
    my_x, even = lax.rem(lax.div(me_ref[0], NC), NX), lax.rem(me_ref[0], NC) == 0
    whole_ref[features:, :] = jnp.zeros((whole_ref.shape[0] - features, 128), F32)
    turned = cot_ref[...].T
    chip = 0
    for i in range(BLOCKS):
        copies[i].wait()
        across = jnp.dot(
            turned, tokens_ref[:, i * width : i * width + width], preferred_element_type=F32
        )
        whole_ref[i * width : i * width + width, :] = across.T
        ready = (i + 1) * width if i < BLOCKS - 1 else whole_ref.shape[0]
        while chip < DP // NC and (2 * chip + 1) * rows_dev + PAD <= ready:
            z, x = chip // NX, chip % NX
            apart = jnp.bitwise_xor(my_x, x)
            zero, one = pick_of(apart, (18, 6, 0, 12)), pick_of(apart, (18, 12, 0, 6))
            kept = z + jnp.where(even, zero, one)
            sent = z + jnp.where(even, one, zero)
            first = whole_ref[2 * chip * rows_dev : 2 * chip * rows_dev + PAD, :]
            second = whole_ref[(2 * chip + 1) * rows_dev : (2 * chip + 1) * rows_dev + PAD, :]
            keep_ref[kept] = jnp.where(even, first, second)
            send_ref[sent] = jnp.where(even, second, first).astype(BF16)
            chip += 1


def grad(me, cotangent, tokens, rows_dev):
    _, features = tokens.shape
    return pl.pallas_call(
        functools.partial(grad_kernel, rows_dev),
        out_shape=(
            jax.ShapeDtypeStruct((24, PAD, 128), BF16),
            jax.ShapeDtypeStruct((24, PAD, 128), F32),
        ),
        in_specs=[
            pl.BlockSpec(memory_space=pltpu.SMEM),
            pl.BlockSpec(memory_space=pltpu.VMEM),
            pl.BlockSpec(memory_space=pltpu.HBM),
        ],
        out_specs=[pl.BlockSpec(memory_space=pltpu.VMEM)] * 2,
        scratch_shapes=[
            pltpu.VMEM(tokens.shape, BF16),
            pltpu.VMEM((features + 32, 128), F32),
            pltpu.SemaphoreType.DMA((BLOCKS,)),
        ],
        compiler_params=pltpu.CompilerParams(vmem_limit_bytes=60_000_000),
        name="grad",
    )(me.reshape(1), cotangent, tokens)


def apply_kernel(
    rows_dev, me_ref, mine_ref, other_ref, tokens_hbm, out_ref, tokens_ref, rows_ref, sems
):
    features = tokens_ref.shape[1]
    width = features // BLOCKS
    copies = fetch(tokens_hbm, tokens_ref, sems)
    my_x, even = lax.rem(lax.div(me_ref[0], NC), NX), lax.rem(me_ref[0], NC) == 0
    total = jnp.zeros(out_ref.shape, F32)
    chip = 0
    for i in range(BLOCKS):
        while chip < DP // NC and 2 * chip * rows_dev < (i + 1) * width:
            z, x = chip // NX, chip % NX
            apart = jnp.bitwise_xor(my_x, x)
            zero, one = pick_of(apart, (0, 6, 18, 12)), pick_of(apart, (0, 12, 18, 6))
            mine = mine_ref[z + jnp.where(even, zero, one)].astype(F32)
            other = other_ref[z + jnp.where(even, one, zero)].astype(F32)
            start = 2 * chip * rows_dev
            rows_ref[start : start + PAD, :] = jnp.where(even, mine, other)
            start += rows_dev
            rows_ref[start : start + PAD, :] = jnp.where(even, other, mine)
            chip += 1
        block = slice(i * width, i * width + width)
        copies[i].wait()
        total += jnp.dot(
            tokens_ref[:, block], rows_ref[block, :].astype(BF16), preferred_element_type=F32
        )
    out_ref[...] = total.astype(BF16)


def apply(me, mine, other, tokens, rows_dev):
    tall, features = tokens.shape
    return pl.pallas_call(
        functools.partial(apply_kernel, rows_dev),
        out_shape=jax.ShapeDtypeStruct((tall, 128), BF16),
        in_specs=[pl.BlockSpec(memory_space=pltpu.SMEM)]
        + [pl.BlockSpec(memory_space=pltpu.VMEM)] * 2
        + [pl.BlockSpec(memory_space=pltpu.HBM)],
        scratch_shapes=[
            pltpu.VMEM(tokens.shape, BF16),
            pltpu.VMEM((features + 32, 128), F32),
            pltpu.SemaphoreType.DMA((BLOCKS,)),
        ],
        compiler_params=pltpu.CompilerParams(vmem_limit_bytes=60_000_000),
        name="apply",
    )(me.reshape(1), mine, other, tokens)


def per_device(tokens, cotangent, master, first_moment, second_moment, old_rows):
    rows_dev = master.shape[0]
    me = lax.axis_index("dp")

    send, keep = grad(me, cotangent, tokens, rows_dev)
    got = shift(send, dc=1)
    next_x = (keep[:12] + got[:12].astype(F32)).astype(BF16)

    box = route(old_rows, master, first_moment, second_moment)
    got_x = shift(next_x, dx=FIRST)
    arrived = lax.all_to_all(box, "dp", split_axis=0, concat_axis=0, tiled=True)
    weight_own, first, second = place(arrived)

    next_x = keep[12:18] + got[12:18].astype(F32) + got_x[:6].astype(F32)
    next_x = next_x.astype(BF16)
    next_x, got_x = lax.optimization_barrier((next_x, got_x))
    last_x = shift(next_x, dx=SECOND)
    sums = (
        keep[18:] + got[18:].astype(F32) + got_x[6:].astype(F32) + last_x.astype(F32)
    )
    got_z = along_z(sums.astype(BF16))
    gradient = jnp.sum(got_z.astype(F32), axis=0)[:rows_dev]

    squares = jnp.sum(gradient * gradient)
    high = squares.astype(BF16)
    middle = (squares - high.astype(F32)).astype(BF16)
    low = (squares - high.astype(F32) - middle.astype(F32)).astype(BF16)
    row = lax.broadcasted_iota(jnp.int32, (PAD, 128), 0)
    own = jnp.where(
        row < rows_dev,
        weight_own,
        jnp.where(row == rows_dev, high, jnp.where(row == rows_dev + 1, middle, low)),
    )

    run = along_z(jnp.broadcast_to(own, (NZ, PAD, 128)))
    pair = jnp.concatenate([run, shift(run, dx=FIRST)], axis=0)
    mine = jnp.concatenate([pair, shift(pair, dx=SECOND)], axis=0)
    other = shift(mine, dc=1)

    ends = slice(rows_dev, rows_dev + 3)
    squares = jnp.sum(mine[:, ends, :].astype(F32) + other[:, ends, :].astype(F32), axis=(0, 1))
    copies = jnp.broadcast_to(squares, (lax.axis_size("tensor"), 8, 128))
    parts = lax.all_to_all(copies, "tensor", split_axis=0, concat_axis=0, tiled=True)
    keys_values = apply(me, mine, other, tokens, rows_dev)
    keys_values, parts = lax.optimization_barrier((keys_values, parts))
    squares = jnp.sum(parts[:, 0, 0])

    factor = clip_norm / (jnp.sqrt(squares) + 1e-06)
    clipped = gradient * factor
    moment_one = beta_one * first[:rows_dev] + (1.0 - beta_one) * clipped
    moment_two = beta_two * second[:rows_dev] + (1.0 - beta_two) * clipped * clipped
    update = moment_one / (jnp.sqrt(moment_two) + adam_eps)
    return (keys_values, update)


def solution(mesh):
    in_specs = (
        P("dp", None),
        P("dp", "tensor"),
        P("dp", "tensor"),
        P("dp", "tensor"),
        P("dp", "tensor"),
        P("dp"),
    )
    out_specs = (P("dp", "tensor"), P("dp", "tensor"))
    return jax.shard_map(
        per_device, mesh=mesh, in_specs=in_specs, out_specs=out_specs, check_vma=False
    )
```

profile of v0, /device:TPU:1, one launch (start us, length us, event | category | flops | bytes accessed | tf_op | source)
XLA Modules:
  0.0 151.4 jit_solution(10683863509152823335)
XLA Ops:
  0.6 7.5 %grad.1 = (bf16[24,176,128]{2,1,0:T(8,128)(2,1)}, f32[24,176,128]{2,1,0:T(8,128)}) custom-call(s32[1]{0:T(128)} %bitcast.me_ref, bf16[512,128]{1,0:T(8,128)(2,1)} %cot_ref.1, bf16[512,8192]{1,0:T(8,128)(2,1)} %tokens_hbm.3), custom_call_target="tpu_custom_call" | custom-call | tf_op jit(solution)/shard_map/grad/pallas_call | solution.py:165
  8.2 12.4 %collective-permute-start = (bf16[24,176,128]{2,1,0:T(8,128)(2,1)}, bf16[24,176,128]{2,1,0:T(8,128)(2,1)S(1)}, u32[]{:S(2)}, u32[]{:S(2)}) collective-permute-start(bf16[24,176,128]{2,1,0:T(8,128)(2,1)} %get-tuple-element.13), channel_id=1, source_target_pairs={{0,16},{16,0},{32,48},{48,32},{64,80},{80,64},{96,112},{112,96},{1... | collective-permute-start | bytes 3244040 | tf_op jit(solution)/shard_map/ppermute | solution.py:33
  20.6 2.5 %collective-permute-done = bf16[24,176,128]{2,1,0:T(8,128)(2,1)S(1)} collective-permute-done((bf16[24,176,128]{2,1,0:T(8,128)(2,1)}, bf16[24,176,128]{2,1,0:T(8,128)(2,1)S(1)}, u32[]{:S(2)}, u32[]{:S(2)}) %collective-permute-start) | collective-permute-done | bytes 1081376 | tf_op jit(solution)/shard_map/ppermute | solution.py:33
  23.1 2.6 %add_convert_fusion = bf16[12,176,128]{2,1,0:T(8,128)(2,1)} fusion(f32[24,176,128]{2,1,0:T(8,128)} %get-tuple-element.12, bf16[24,176,128]{2,1,0:T(8,128)(2,1)S(1)} %collective-permute-done), kind=kLoop, calls=%fused_computation | loop fusion | flops 811008 | bytes 2162688 | tf_op jit(solution)/shard_map/convert_element_type | solution.py:240
  25.7 1.9 %collective-permute-start.1 = (bf16[12,176,128]{2,1,0:T(8,128)(2,1)}, bf16[12,176,128]{2,1,0:T(8,128)(2,1)S(1)}, u32[]{:S(2)}, u32[]{:S(2)}) collective-permute-start(bf16[12,176,128]{2,1,0:T(8,128)(2,1)} %add_convert_fusion), channel_id=1, source_target_pairs={{0,32},{16,112},{32,0},{48,80},{64,96},{80,48},{96,64},{112,16},{1... | collective-permute-start | bytes 1622024 | tf_op jit(solution)/shard_map/ppermute | solution.py:33
  27.6 2.2 %route.1 = bf16[48,32,128]{2,1,0:T(8,128)(2,1)} custom-call(s32[1,171]{1,0:T(1,128)} %bitcast.2, f32[171,128]{1,0:T(8,128)} %master_ref.1, f32[171,128]{1,0:T(8,128)} %first_ref.1, f32[171,128]{1,0:T(8,128)} %second_ref.1), custom_call_target="tpu_custom_call" | custom-call | tf_op jit(solution)/shard_map/route/pallas_call | solution.py:74
  29.8 7.5 %all-to-all-start = ((bf16[48,32,128]{2,1,0:T(8,128)(2,1)}), bf16[48,32,128]{2,1,0:T(8,128)(2,1)S(1)}, u32[]{:S(2)}, u32[]{:S(2)}) async-start(bf16[48,32,128]{2,1,0:T(8,128)(2,1)} %route.1), calls=%async_computation | async-start | bytes 786432 | tf_op jit(solution)/shard_map/all_to_all | solution.py:244
  38.3 3.3 %collective-permute-start.2 = (bf16[6,176,128]{2,1,0:T(8,128)(2,1)S(1)}, bf16[6,176,128]{2,1,0:T(8,128)(2,1)S(1)}, u32[]{:S(2)}, u32[]{:S(2)}) collective-permute-start(bf16[6,176,128]{2,1,0:T(8,128)(2,1)S(1)} %add_convert_fusion.2), channel_id=1, source_target_pairs={{0,96},{16,48},{32,64},{48,16},{64,32},{80,112},{96,0},{112,80},{1... | collective-permute-start | bytes 811016 | tf_op jit(solution)/shard_map/ppermute | solution.py:33
  41.6 5.2 %collective-permute-done.2 = bf16[6,176,128]{2,1,0:T(8,128)(2,1)S(1)} collective-permute-done((bf16[6,176,128]{2,1,0:T(8,128)(2,1)S(1)}, bf16[6,176,128]{2,1,0:T(8,128)(2,1)S(1)}, u32[]{:S(2)}, u32[]{:S(2)}) %collective-permute-start.2) | collective-permute-done | bytes 270368 | tf_op jit(solution)/shard_map/ppermute | solution.py:33
  46.8 1.8 %add_convert_fusion.1 = bf16[6,176,128]{2,1,0:T(8,128)(2,1)} fusion(bf16[6,176,128]{2,1,0:T(8,128)(2,1)S(1)} %collective-permute-done.2, f32[24,176,128]{2,1,0:T(8,128)S(1)} %copy-done, bf16[24,176,128]{2,1,0:T(8,128)(2,1)} %copy-done.4, bf16[12,176,128]{2,1,0:T(8,128)(2,1)S(1)} %collective-permute-done.1), kind=kLoop, calls=%fused_computation.3 | loop fusion | flops 946176 | bytes 1622016 | tf_op jit(solution)/shard_map/convert_element_type | solution.py:254
  48.6 5.8 %all-to-all-done.box_ref = bf16[48,32,128]{2,1,0:T(8,128)(2,1)S(1)} async-done(((bf16[48,32,128]{2,1,0:T(8,128)(2,1)}), bf16[48,32,128]{2,1,0:T(8,128)(2,1)S(1)}, u32[]{:S(2)}, u32[]{:S(2)}) %all-to-all-start) | async-done | bytes 393248 | tf_op jit(solution)/shard_map/all_to_all | solution.py:244
  54.5 6.5 %all-to-all-start.1 = ((bf16[6,176,128]{2,1,0:T(8,128)(2,1)}), bf16[6,176,128]{2,1,0:T(8,128)(2,1)S(1)}, u32[]{:S(2)}, u32[]{:S(2)}) async-start(bf16[6,176,128]{2,1,0:T(8,128)(2,1)} %add_convert_fusion.1), calls=%async_computation.1 | async-start | bytes 540672 | tf_op jit(solution)/shard_map/all_to_all | solution.py:39
  61.0 2.0 %place.1 = (bf16[176,128]{1,0:T(8,128)(2,1)}, f32[176,128]{1,0:T(8,128)}, f32[176,128]{1,0:T(8,128)}) custom-call(bf16[48,32,128]{2,1,0:T(8,128)(2,1)} %copy-done.2), custom_call_target="tpu_custom_call" | custom-call | tf_op jit(solution)/shard_map/place/pallas_call | solution.py:100
  63.0 11.2 %all-to-all-done.1 = bf16[6,176,128]{2,1,0:T(8,128)(2,1)S(1)} async-done(((bf16[6,176,128]{2,1,0:T(8,128)(2,1)}), bf16[6,176,128]{2,1,0:T(8,128)(2,1)S(1)}, u32[]{:S(2)}, u32[]{:S(2)}) %all-to-all-start.1) | async-done | bytes 270368 | tf_op jit(solution)/shard_map/all_to_all | solution.py:39
  77.0 16.5 %all_to_all.20 = bf16[6,176,128]{2,1,0:T(8,128)(2,1)S(1)} all-to-all(bf16[6,176,128]{2,1,0:T(8,128)(2,1)S(1)} %broadcast_in_dim.21), channel_id=1, replica_groups={{0,128,256,384,512,640},{16,144,272,400,528,656},{32,160,288,416,544,67..., dimensions={0} | all-to-all | bytes 540672 | tf_op jit(solution)/shard_map/all_to_all | solution.py:39
  93.5 2.2 %collective-permute-start.3 = (bf16[6,176,128]{2,1,0:T(8,128)(2,1)S(1)}, bf16[6,176,128]{2,1,0:T(8,128)(2,1)S(1)}, u32[]{:S(2)}, u32[]{:S(2)}) collective-permute-start(bf16[6,176,128]{2,1,0:T(8,128)(2,1)S(1)} %all_to_all.20), channel_id=1, source_target_pairs={{0,32},{16,112},{32,0},{48,80},{64,96},{80,48},{96,64},{112,16},{1... | collective-permute-start | bytes 811016 | tf_op jit(solution)/shard_map/ppermute | solution.py:33
  95.7 6.2 %collective-permute-done.3 = bf16[6,176,128]{2,1,0:T(8,128)(2,1)S(1)} collective-permute-done((bf16[6,176,128]{2,1,0:T(8,128)(2,1)S(1)}, bf16[6,176,128]{2,1,0:T(8,128)(2,1)S(1)}, u32[]{:S(2)}, u32[]{:S(2)}) %collective-permute-start.3) | collective-permute-done | bytes 270368 | tf_op jit(solution)/shard_map/ppermute | solution.py:33
  102.0 1.9 %collective-permute-start.4 = (bf16[12,176,128]{2,1,0:T(8,128)(2,1)S(1)}, bf16[12,176,128]{2,1,0:T(8,128)(2,1)S(1)}, u32[]{:S(2)}, u32[]{:S(2)}) collective-permute-start(bf16[12,176,128]{2,1,0:T(8,128)(2,1)S(1)} %pad_maximum_fusion), channel_id=1, source_target_pairs={{0,96},{16,48},{32,64},{48,16},{64,32},{80,112},{96,0},{112,80},{1... | collective-permute-start | bytes 1622024 | tf_op jit(solution)/shard_map/ppermute | solution.py:33
  104.0 8.4 %collective-permute-done.4 = bf16[12,176,128]{2,1,0:T(8,128)(2,1)S(1)} collective-permute-done((bf16[12,176,128]{2,1,0:T(8,128)(2,1)S(1)}, bf16[12,176,128]{2,1,0:T(8,128)(2,1)S(1)}, u32[]{:S(2)}, u32[]{:S(2)}) %collective-permute-start.4) | collective-permute-done | bytes 540704 | tf_op jit(solution)/shard_map/ppermute | solution.py:33
  112.5 5.6 %collective-permute-start.5 = (bf16[24,176,128]{2,1,0:T(8,128)(2,1)S(1)}, bf16[24,176,128]{2,1,0:T(8,128)(2,1)S(1)}, u32[]{:S(2)}, u32[]{:S(2)}) collective-permute-start(bf16[24,176,128]{2,1,0:T(8,128)(2,1)S(1)} %constant_dynamic-update-slice_fusion.mine_ref), channel_id=1, source_target_pairs={{0,16},{16,0},{32,48},{48,32},{64,80},{80,64},{96,112},{112,96},{1... | collective-permute-start | bytes 3244040 | tf_op jit(solution)/shard_map/ppermute | solution.py:33
  118.1 2.3 %collective-permute-done.5.other_ref = bf16[24,176,128]{2,1,0:T(8,128)(2,1)S(1)} collective-permute-done((bf16[24,176,128]{2,1,0:T(8,128)(2,1)S(1)}, bf16[24,176,128]{2,1,0:T(8,128)(2,1)S(1)}, u32[]{:S(2)}, u32[]{:S(2)}) %collective-permute-start.5) | collective-permute-done | bytes 1081376 | tf_op jit(solution)/shard_map/ppermute | solution.py:33
  121.1 14.5 %all-to-all-start.3 = ((f32[16,8,128]{2,1,0:T(8,128)}), f32[16,8,128]{2,1,0:T(8,128)S(1)}, u32[]{:S(2)}, u32[]{:S(2)}) async-start(f32[16,8,128]{2,1,0:T(8,128)} %broadcast_in_dim.22), calls=%async_computation.3 | async-start | bytes 131072 | tf_op jit(solution)/shard_map/all_to_all | solution.py:276
  135.7 9.0 %apply.1 = bf16[512,128]{1,0:T(8,128)(2,1)} custom-call(s32[1]{0:T(128)} %bitcast.me_ref, bf16[24,176,128]{2,1,0:T(8,128)(2,1)} %copy-done.1, bf16[24,176,128]{2,1,0:T(8,128)(2,1)} %copy-done.3, bf16[512,8192]{1,0:T(8,128)(2,1)} %tokens_hbm.3), custom_call_target="tpu_custom_call" | custom-call | tf_op jit(solution)/shard_map/apply/pallas_call | solution.py:218
  144.7 4.7 %all-to-all-done.3 = f32[16,8,128]{2,1,0:T(8,128)S(1)} async-done(((f32[16,8,128]{2,1,0:T(8,128)}), f32[16,8,128]{2,1,0:T(8,128)S(1)}, u32[]{:S(2)}, u32[]{:S(2)}) %all-to-all-start.3) | async-done | bytes 65568 | tf_op jit(solution)/shard_map/all_to_all | solution.py:276
  (30 shorter events, 5.0 us)
Async XLA Ops:
  8.2 14.9 %collective-permute-start = (bf16[24,176,128]{2,1,0:T(8,128)(2,1)}, bf16[24,176,128]{2,1,0:T(8,128)(2,1)S(1)}, u32[]{:S(2)}, u32[]{:S(2)}) collective-permute-start(bf16[24,176,128]{2,1,0:T(8,128)(2,1)} %get-tuple-element.13), channel_id=1, source_target_pairs={{0,16},{16,0},{32,48},{48,32},{64,80},{80,64},{96,112},{112,96},{1... | collective-permute-start | bytes 3244040 | tf_op jit(solution)/shard_map/ppermute | solution.py:33
  23.1 2.6 %copy-start.4 = (bf16[24,176,128]{2,1,0:T(8,128)(2,1)}, bf16[24,176,128]{2,1,0:T(8,128)(2,1)S(1)}, u32[]{:S(2)}) copy-start(bf16[24,176,128]{2,1,0:T(8,128)(2,1)S(1)} %collective-permute-done) | copy-start | bytes 3244036
  23.1 14.2 %copy-start = (f32[24,176,128]{2,1,0:T(8,128)S(1)}, f32[24,176,128]{2,1,0:T(8,128)}, u32[]{:S(2)}) copy-start(f32[24,176,128]{2,1,0:T(8,128)} %get-tuple-element.12) | copy-start | bytes 6488068
  25.7 11.6 %collective-permute-start.1 = (bf16[12,176,128]{2,1,0:T(8,128)(2,1)}, bf16[12,176,128]{2,1,0:T(8,128)(2,1)S(1)}, u32[]{:S(2)}, u32[]{:S(2)}) collective-permute-start(bf16[12,176,128]{2,1,0:T(8,128)(2,1)} %add_convert_fusion), channel_id=1, source_target_pairs={{0,32},{16,112},{32,0},{48,80},{64,96},{80,48},{96,64},{112,16},{1... | collective-permute-start | bytes 1622024 | tf_op jit(solution)/shard_map/ppermute | solution.py:33
  29.8 24.7 %all-to-all-start = ((bf16[48,32,128]{2,1,0:T(8,128)(2,1)}), bf16[48,32,128]{2,1,0:T(8,128)(2,1)S(1)}, u32[]{:S(2)}, u32[]{:S(2)}) async-start(bf16[48,32,128]{2,1,0:T(8,128)(2,1)} %route.1), calls=%async_computation | async-start | bytes 786432 | tf_op jit(solution)/shard_map/all_to_all | solution.py:244
  38.3 8.5 %collective-permute-start.2 = (bf16[6,176,128]{2,1,0:T(8,128)(2,1)S(1)}, bf16[6,176,128]{2,1,0:T(8,128)(2,1)S(1)}, u32[]{:S(2)}, u32[]{:S(2)}) collective-permute-start(bf16[6,176,128]{2,1,0:T(8,128)(2,1)S(1)} %add_convert_fusion.2), channel_id=1, source_target_pairs={{0,96},{16,48},{32,64},{48,16},{64,32},{80,112},{96,0},{112,80},{1... | collective-permute-start | bytes 811016 | tf_op jit(solution)/shard_map/ppermute | solution.py:33
  54.4 6.5 %copy-start.2 = (bf16[48,32,128]{2,1,0:T(8,128)(2,1)}, bf16[48,32,128]{2,1,0:T(8,128)(2,1)S(1)}, u32[]{:S(2)}) copy-start(bf16[48,32,128]{2,1,0:T(8,128)(2,1)S(1)} %all-to-all-done.box_ref) | copy-start | bytes 1179652
  54.5 19.8 %all-to-all-start.1 = ((bf16[6,176,128]{2,1,0:T(8,128)(2,1)}), bf16[6,176,128]{2,1,0:T(8,128)(2,1)S(1)}, u32[]{:S(2)}, u32[]{:S(2)}) async-start(bf16[6,176,128]{2,1,0:T(8,128)(2,1)} %add_convert_fusion.1), calls=%async_computation.1 | async-start | bytes 540672 | tf_op jit(solution)/shard_map/all_to_all | solution.py:39
  93.5 8.4 %collective-permute-start.3 = (bf16[6,176,128]{2,1,0:T(8,128)(2,1)S(1)}, bf16[6,176,128]{2,1,0:T(8,128)(2,1)S(1)}, u32[]{:S(2)}, u32[]{:S(2)}) collective-permute-start(bf16[6,176,128]{2,1,0:T(8,128)(2,1)S(1)} %all_to_all.20), channel_id=1, source_target_pairs={{0,32},{16,112},{32,0},{48,80},{64,96},{80,48},{96,64},{112,16},{1... | collective-permute-start | bytes 811016 | tf_op jit(solution)/shard_map/ppermute | solution.py:33
  102.0 10.4 %collective-permute-start.4 = (bf16[12,176,128]{2,1,0:T(8,128)(2,1)S(1)}, bf16[12,176,128]{2,1,0:T(8,128)(2,1)S(1)}, u32[]{:S(2)}, u32[]{:S(2)}) collective-permute-start(bf16[12,176,128]{2,1,0:T(8,128)(2,1)S(1)} %pad_maximum_fusion), channel_id=1, source_target_pairs={{0,96},{16,48},{32,64},{48,16},{64,32},{80,112},{96,0},{112,80},{1... | collective-permute-start | bytes 1622024 | tf_op jit(solution)/shard_map/ppermute | solution.py:33
  112.4 23.2 %copy-start.1 = (bf16[24,176,128]{2,1,0:T(8,128)(2,1)}, bf16[24,176,128]{2,1,0:T(8,128)(2,1)S(1)}, u32[]{:S(2)}) copy-start(bf16[24,176,128]{2,1,0:T(8,128)(2,1)S(1)} %constant_dynamic-update-slice_fusion.mine_ref) | copy-start | bytes 3244036
  112.5 7.9 %collective-permute-start.5 = (bf16[24,176,128]{2,1,0:T(8,128)(2,1)S(1)}, bf16[24,176,128]{2,1,0:T(8,128)(2,1)S(1)}, u32[]{:S(2)}, u32[]{:S(2)}) collective-permute-start(bf16[24,176,128]{2,1,0:T(8,128)(2,1)S(1)} %constant_dynamic-update-slice_fusion.mine_ref), channel_id=1, source_target_pairs={{0,16},{16,0},{32,48},{48,32},{64,80},{80,64},{96,112},{112,96},{1... | collective-permute-start | bytes 3244040 | tf_op jit(solution)/shard_map/ppermute | solution.py:33
  120.4 15.3 %copy-start.3 = (bf16[24,176,128]{2,1,0:T(8,128)(2,1)}, bf16[24,176,128]{2,1,0:T(8,128)(2,1)S(1)}, u32[]{:S(2)}) copy-start(bf16[24,176,128]{2,1,0:T(8,128)(2,1)S(1)} %collective-permute-done.5.other_ref) | copy-start | bytes 3244036
  121.1 28.2 %all-to-all-start.3 = ((f32[16,8,128]{2,1,0:T(8,128)}), f32[16,8,128]{2,1,0:T(8,128)S(1)}, u32[]{:S(2)}, u32[]{:S(2)}) async-start(f32[16,8,128]{2,1,0:T(8,128)} %broadcast_in_dim.22), calls=%async_computation.3 | async-start | bytes 131072 | tf_op jit(solution)/shard_map/all_to_all | solution.py:276
  135.7 15.0 %copy-start.5 = (f32[176,128]{1,0:T(8,128)S(1)}, f32[176,128]{1,0:T(8,128)}, u32[]{:S(2)}) copy-start(f32[176,128]{1,0:T(8,128)} %get-tuple-element.17) | copy-start | bytes 270340
  135.7 15.0 %copy-start.6 = (f32[176,128]{1,0:T(8,128)S(1)}, f32[176,128]{1,0:T(8,128)}, u32[]{:S(2)}) copy-start(f32[176,128]{1,0:T(8,128)} %get-tuple-element.19) | copy-start | bytes 270340
where the time goes:
time: 152 us; the launch traced here: 151 us
  starting transfers between devices  55.8 us (37%)
  waiting for transfers between devices  46.4 us (31%)
  Pallas kernels  20.6 us (14%)
  blocking collectives  16.5 us (11%)
  other arithmetic  8.44 us (6%)
  between operations  2.73 us (2%)
    ppermute x6, starting transfers between devices, shift(): return lax.ppermute(value, 'dp', pairs)  27.3 us
    ppermute x6, waiting for transfers between devices, shift(): return lax.ppermute(value, 'dp', pairs)  24.6 us
    all_to_all x1, blocking collectives, along_z(): lax.all_to_all(value, 'dp', split_axis=0, concat_axis=0, tiled=True, axis...  16.5 us
    all_to_all x1, starting transfers between devices, per_device(): lax.all_to_all(copies, 'tensor', split_axis=0, concat_axis=0, tiled=True)  14.5 us
    all_to_all x1, waiting for transfers between devices, along_z(): lax.all_to_all(value, 'dp', split_axis=0, concat_axis=0, tiled=True, axis...  11.2 us
    pallas_call x1, Pallas kernels, apply(): pl.pallas_call(functools.partial(apply_kernel, rows_dev), out_shape=jax.S...  8.95 us
    pallas_call x1, Pallas kernels, grad(): pl.pallas_call(functools.partial(grad_kernel, rows_dev), out_shape=(jax.S...  7.51 us
    all_to_all x1, starting transfers between devices, per_device(): arrived = lax.all_to_all(box, 'dp', split_axis=0, concat_axis=0, tiled=True)  7.49 us
  transfers between devices with their start and end apart: 9, of which 8 were waited for; matrix products, arithmetic and copies ran while one was open for 2% of the time, Pallas kernels for 9%

commit v1 on v0

--- a/solution.py
+++ b/solution.py
@@ -39,6 +39,12 @@
     return lax.all_to_all(
         value, "dp", split_axis=0, concat_axis=0, tiled=True, axis_index_groups=groups
     )
+
+
+def sum_over(value, axis):
+    copies = jnp.broadcast_to(value, (lax.axis_size(axis), 8, 128))
+    parts = lax.all_to_all(copies, axis, split_axis=0, concat_axis=0, tiled=True)
+    return jnp.sum(parts[:, 0, 0])
 
 
 def iota(shape, axis):
@@ -91,7 +97,9 @@
     placed = lax.dot_general(
         pick, data, (((0,), (0,)), ((), ())), preferred_element_type=F32
     )
-    weight_ref[...] = placed[:PAD, :128].astype(BF16)
+    weight = placed[:PAD, :128].astype(BF16)
+    for z in range(NZ):
+        weight_ref[z] = weight
     first_ref[...] = placed[:PAD, 128:256]
     second_ref[...] = placed[:PAD, 256:384]
 
@@ -100,7 +108,7 @@
     return pl.pallas_call(
         place_kernel,
         out_shape=(
-            jax.ShapeDtypeStruct((PAD, 128), BF16),
+            jax.ShapeDtypeStruct((NZ, PAD, 128), BF16),
             jax.ShapeDtypeStruct((PAD, 128), F32),
             jax.ShapeDtypeStruct((PAD, 128), F32),
         ),
@@ -235,48 +243,33 @@
     rows_dev = master.shape[0]
     me = lax.axis_index("dp")
 
+    box = route(old_rows, master, first_moment, second_moment)
+    arrived = lax.all_to_all(box, "dp", split_axis=0, concat_axis=0, tiled=True)
+    weight_own, first, second = place(arrived)
+
     send, keep = grad(me, cotangent, tokens, rows_dev)
     got = shift(send, dc=1)
     next_x = (keep[:12] + got[:12].astype(F32)).astype(BF16)
-
-    box = route(old_rows, master, first_moment, second_moment)
     got_x = shift(next_x, dx=FIRST)
-    arrived = lax.all_to_all(box, "dp", split_axis=0, concat_axis=0, tiled=True)
-    weight_own, first, second = place(arrived)
-
     next_x = keep[12:18] + got[12:18].astype(F32) + got_x[:6].astype(F32)
     next_x = next_x.astype(BF16)
     next_x, got_x = lax.optimization_barrier((next_x, got_x))
     last_x = shift(next_x, dx=SECOND)
-    sums = (
-        keep[18:] + got[18:].astype(F32) + got_x[6:].astype(F32) + last_x.astype(F32)
-    )
+    sums = keep[18:] + got[18:].astype(F32) + got_x[6:].astype(F32) + last_x.astype(F32)
     got_z = along_z(sums.astype(BF16))
     gradient = jnp.sum(got_z.astype(F32), axis=0)[:rows_dev]
 
+    run = along_z(weight_own)
+    west = shift(run, dx=FIRST)
+    pair = jnp.concatenate([run, west], axis=0)
+    rest = shift(pair, dx=SECOND)
+    mine = jnp.concatenate([pair, rest], axis=0)
+    other = shift(mine, dc=1)
+
     squares = jnp.sum(gradient * gradient)
-    high = squares.astype(BF16)
-    middle = (squares - high.astype(F32)).astype(BF16)
-    low = (squares - high.astype(F32) - middle.astype(F32)).astype(BF16)
-    row = lax.broadcasted_iota(jnp.int32, (PAD, 128), 0)
-    own = jnp.where(
-        row < rows_dev,
-        weight_own,
-        jnp.where(row == rows_dev, high, jnp.where(row == rows_dev + 1, middle, low)),
-    )
-
-    run = along_z(jnp.broadcast_to(own, (NZ, PAD, 128)))
-    pair = jnp.concatenate([run, shift(run, dx=FIRST)], axis=0)
-    mine = jnp.concatenate([pair, shift(pair, dx=SECOND)], axis=0)
-    other = shift(mine, dc=1)
-
-    ends = slice(rows_dev, rows_dev + 3)
-    squares = jnp.sum(mine[:, ends, :].astype(F32) + other[:, ends, :].astype(F32), axis=(0, 1))
-    copies = jnp.broadcast_to(squares, (lax.axis_size("tensor"), 8, 128))
-    parts = lax.all_to_all(copies, "tensor", split_axis=0, concat_axis=0, tiled=True)
+    squares = sum_over(squares, "tensor")
+    squares = sum_over(squares, "dp")
     keys_values = apply(me, mine, other, tokens, rows_dev)
-    keys_values, parts = lax.optimization_barrier((keys_values, parts))
-    squares = jnp.sum(parts[:, 0, 0])
 
     factor = clip_norm / (jnp.sqrt(squares) + 1e-06)
     clipped = gradient * factor

time: 152 us -> 157 us (1.033)
  waiting for transfers between devices: 46.4 us -> 30.8 us
  blocking collectives: 16.5 us -> 28.4 us
  starting transfers between devices: 55.8 us -> 61.4 us
  local copies, waits for them, and re-layouts: 0.92 us -> 4.8 us
    ppermute x6, waiting for transfers between devices: 24.6 us -> 11.8 us  [shift(): return lax.ppermute(value, 'dp', pairs)]
    all_to_all x1, blocking collectives: 16.5 us -> 28.4 us  [sum_over(): lax.all_to_all(copies, axis, split_axis=0, concat_axis=0, tiled=True)]
    all_to_all x1 -> x2, waiting for transfers between devices: 11.2 us -> 2.88 us  [along_z(): lax.all_to_all(value, 'dp', split_axis=0, concat_axis=0, tiled=True, axis...]
    all_to_all x1 -> x2, starting transfers between devices: 6.53 us -> 11.2 us  [along_z(): lax.all_to_all(value, 'dp', split_axis=0, concat_axis=0, tiled=True, axis...]
    all_to_all x1, waiting for transfers between devices: 5.85 us -> 9.3 us  [per_device(): arrived = lax.all_to_all(box, 'dp', split_axis=0, concat_axis=0, tiled=True)]
    unnamed x16, local copies, waits for them, and re-layouts: 0.09 us -> 2.8 us
    ppermute x6, starting transfers between devices: 27.3 us -> 29.6 us  [shift(): return lax.ppermute(value, 'dp', pairs)]
    all_to_all x1, waiting for transfers between devices: 4.68 us -> 6.85 us  [sum_over(): lax.all_to_all(copies, axis, split_axis=0, concat_axis=0, tiled=True)]
  transfers between devices with their start and end apart: 9 -> 10, of which waited for: 8 -> 5; matrix products, arithmetic and copies ran while one was open for 2% -> 7% of each run, Pallas kernels for 9% -> 3%
where the time goes in v1:
time: 157 us; the launch traced here: 156 us
  starting transfers between devices  61.4 us (39%)
  waiting for transfers between devices  30.8 us (20%)
  blocking collectives  28.4 us (18%)
  Pallas kernels  20.7 us (13%)
  other arithmetic  8.94 us (6%)
  local copies, waits for them, and re-layouts  4.8 us (3%)
    ppermute x6, starting transfers between devices, shift(): return lax.ppermute(value, 'dp', pairs)  29.6 us
    all_to_all x1, blocking collectives, sum_over(): lax.all_to_all(copies, axis, split_axis=0, concat_axis=0, tiled=True)  28.4 us
    all_to_all x1, starting transfers between devices, sum_over(): lax.all_to_all(copies, axis, split_axis=0, concat_axis=0, tiled=True)  14.5 us
    ppermute x6, waiting for transfers between devices, shift(): return lax.ppermute(value, 'dp', pairs)  11.8 us
    all_to_all x2, starting transfers between devices, along_z(): lax.all_to_all(value, 'dp', split_axis=0, concat_axis=0, tiled=True, axis...  11.2 us
    all_to_all x1, waiting for transfers between devices, per_device(): arrived = lax.all_to_all(box, 'dp', split_axis=0, concat_axis=0, tiled=True)  9.3 us
    pallas_call x1, Pallas kernels, apply(): pl.pallas_call(functools.partial(apply_kernel, rows_dev), out_shape=jax.S...  8.91 us
    pallas_call x1, Pallas kernels, grad(): pl.pallas_call(functools.partial(grad_kernel, rows_dev), out_shape=(jax.S...  7.51 us
  transfers between devices with their start and end apart: 10, of which 5 were waited for; matrix products, arithmetic and copies ran while one was open for 7% of the time, Pallas kernels for 3%

profile of v1, /device:TPU:1, one launch (start us, length us, event | category | flops | bytes accessed | tf_op | source)
XLA Modules:
  0.0 156.5 jit_solution(1955086159981616419)
XLA Ops:
  0.6 7.5 %grad.1 = (bf16[24,176,128]{2,1,0:T(8,128)(2,1)}, f32[24,176,128]{2,1,0:T(8,128)}) custom-call(s32[1]{0:T(128)} %bitcast.me_ref, bf16[512,128]{1,0:T(8,128)(2,1)} %cot_ref.1, bf16[512,8192]{1,0:T(8,128)(2,1)} %tokens_hbm.3), custom_call_target="tpu_custom_call" | custom-call | tf_op jit(solution)/shard_map/grad/pallas_call | solution.py:173
  8.2 12.4 %collective-permute-start.3 = (bf16[24,176,128]{2,1,0:T(8,128)(2,1)}, bf16[24,176,128]{2,1,0:T(8,128)(2,1)S(1)}, u32[]{:S(2)}, u32[]{:S(2)}) collective-permute-start(bf16[24,176,128]{2,1,0:T(8,128)(2,1)} %get-tuple-element.12), channel_id=1, source_target_pairs={{0,16},{16,0},{32,48},{48,32},{64,80},{80,64},{96,112},{112,96},{1... | collective-permute-start | bytes 3244040 | tf_op jit(solution)/shard_map/ppermute | solution.py:33
  20.5 2.2 %route.1 = bf16[48,32,128]{2,1,0:T(8,128)(2,1)} custom-call(s32[1,171]{1,0:T(1,128)} %bitcast.2, f32[171,128]{1,0:T(8,128)} %master_ref.1, f32[171,128]{1,0:T(8,128)} %first_ref.1, f32[171,128]{1,0:T(8,128)} %second_ref.1), custom_call_target="tpu_custom_call" | custom-call | tf_op jit(solution)/shard_map/route/pallas_call | solution.py:80
  22.7 6.0 %all-to-all-start = ((bf16[48,32,128]{2,1,0:T(8,128)(2,1)}), bf16[48,32,128]{2,1,0:T(8,128)(2,1)S(1)}, u32[]{:S(2)}, u32[]{:S(2)}) async-start(bf16[48,32,128]{2,1,0:T(8,128)(2,1)} %route.1), calls=%async_computation | async-start | bytes 786432 | tf_op jit(solution)/shard_map/all_to_all | solution.py:247
  29.8 2.4 %add_convert_fusion = bf16[12,176,128]{2,1,0:T(8,128)(2,1)} fusion(f32[24,176,128]{2,1,0:T(8,128)} %get-tuple-element.11, bf16[24,176,128]{2,1,0:T(8,128)(2,1)} %copy-done.3), kind=kLoop, calls=%fused_computation | loop fusion | flops 811008 | bytes 2162688 | tf_op jit(solution)/shard_map/convert_element_type | solution.py:252
  32.2 4.5 %collective-permute-start.4 = (bf16[12,176,128]{2,1,0:T(8,128)(2,1)}, bf16[12,176,128]{2,1,0:T(8,128)(2,1)S(1)}, u32[]{:S(2)}, u32[]{:S(2)}) collective-permute-start(bf16[12,176,128]{2,1,0:T(8,128)(2,1)} %add_convert_fusion), channel_id=1, source_target_pairs={{0,32},{16,112},{32,0},{48,80},{64,96},{80,48},{96,64},{112,16},{1... | collective-permute-start | bytes 1622024 | tf_op jit(solution)/shard_map/ppermute | solution.py:33
  36.7 9.3 %all-to-all-done.box_ref = bf16[48,32,128]{2,1,0:T(8,128)(2,1)S(1)} async-done(((bf16[48,32,128]{2,1,0:T(8,128)(2,1)}), bf16[48,32,128]{2,1,0:T(8,128)(2,1)S(1)}, u32[]{:S(2)}, u32[]{:S(2)}) %all-to-all-start) | async-done | bytes 393248 | tf_op jit(solution)/shard_map/all_to_all | solution.py:247
  46.7 2.1 %place.1 = (bf16[6,176,128]{2,1,0:T(8,128)(2,1)}, f32[176,128]{1,0:T(8,128)}, f32[176,128]{1,0:T(8,128)}) custom-call(bf16[48,32,128]{2,1,0:T(8,128)(2,1)} %copy-done.2), custom_call_target="tpu_custom_call" | custom-call | tf_op jit(solution)/shard_map/place/pallas_call | solution.py:108
  48.8 6.5 %all-to-all-start.1 = ((bf16[6,176,128]{2,1,0:T(8,128)(2,1)}), bf16[6,176,128]{2,1,0:T(8,128)(2,1)S(1)}, u32[]{:S(2)}, u32[]{:S(2)}) async-start(bf16[6,176,128]{2,1,0:T(8,128)(2,1)} %get-tuple-element.9), calls=%async_computation.1 | async-start | bytes 540672 | tf_op jit(solution)/shard_map/all_to_all | solution.py:39
  56.4 1.9 %collective-permute-start.5 = (bf16[6,176,128]{2,1,0:T(8,128)(2,1)S(1)}, bf16[6,176,128]{2,1,0:T(8,128)(2,1)S(1)}, u32[]{:S(2)}, u32[]{:S(2)}) collective-permute-start(bf16[6,176,128]{2,1,0:T(8,128)(2,1)S(1)} %add_convert_fusion.2), channel_id=1, source_target_pairs={{0,96},{16,48},{32,64},{48,16},{64,32},{80,112},{96,0},{112,80},{1... | collective-permute-start | bytes 811016 | tf_op jit(solution)/shard_map/ppermute | solution.py:33
  58.3 5.6 %collective-permute-done.5 = bf16[6,176,128]{2,1,0:T(8,128)(2,1)S(1)} collective-permute-done((bf16[6,176,128]{2,1,0:T(8,128)(2,1)S(1)}, bf16[6,176,128]{2,1,0:T(8,128)(2,1)S(1)}, u32[]{:S(2)}, u32[]{:S(2)}) %collective-permute-start.5) | collective-permute-done | bytes 270368 | tf_op jit(solution)/shard_map/ppermute | solution.py:33
  63.9 1.8 %add_convert_fusion.1 = bf16[6,176,128]{2,1,0:T(8,128)(2,1)} fusion(bf16[6,176,128]{2,1,0:T(8,128)(2,1)S(1)} %collective-permute-done.5, f32[24,176,128]{2,1,0:T(8,128)S(1)} %copy-done, bf16[24,176,128]{2,1,0:T(8,128)(2,1)} %copy-done.3, bf16[12,176,128]{2,1,0:T(8,128)(2,1)S(1)} %collective-permute-done.4), kind=kLoop, calls=%fused_computation.3 | loop fusion | flops 946176 | bytes 1622016 | tf_op jit(solution)/shard_map/convert_element_type | solution.py:259
  65.7 2.9 %all-to-all-done.1 = bf16[6,176,128]{2,1,0:T(8,128)(2,1)S(1)} async-done(((bf16[6,176,128]{2,1,0:T(8,128)(2,1)}), bf16[6,176,128]{2,1,0:T(8,128)(2,1)S(1)}, u32[]{:S(2)}, u32[]{:S(2)}) %all-to-all-start.1) | async-done | bytes 270368 | tf_op jit(solution)/shard_map/all_to_all | solution.py:39
  68.6 4.7 %all-to-all-start.2 = ((bf16[6,176,128]{2,1,0:T(8,128)(2,1)}), bf16[6,176,128]{2,1,0:T(8,128)(2,1)S(1)}, u32[]{:S(2)}, u32[]{:S(2)}) async-start(bf16[6,176,128]{2,1,0:T(8,128)(2,1)} %add_convert_fusion.1), calls=%async_computation.2 | async-start | bytes 540672 | tf_op jit(solution)/shard_map/all_to_all | solution.py:39
  73.2 2.2 %collective-permute-start = (bf16[6,176,128]{2,1,0:T(8,128)(2,1)S(1)}, bf16[6,176,128]{2,1,0:T(8,128)(2,1)S(1)}, u32[]{:S(2)}, u32[]{:S(2)}) collective-permute-start(bf16[6,176,128]{2,1,0:T(8,128)(2,1)S(1)} %all-to-all-done.1), channel_id=1, source_target_pairs={{0,32},{16,112},{32,0},{48,80},{64,96},{80,48},{96,64},{112,16},{1... | collective-permute-start | bytes 811016 | tf_op jit(solution)/shard_map/ppermute | solution.py:33
  75.5 6.2 %collective-permute-done = bf16[6,176,128]{2,1,0:T(8,128)(2,1)S(1)} collective-permute-done((bf16[6,176,128]{2,1,0:T(8,128)(2,1)S(1)}, bf16[6,176,128]{2,1,0:T(8,128)(2,1)S(1)}, u32[]{:S(2)}, u32[]{:S(2)}) %collective-permute-start) | collective-permute-done | bytes 270368 | tf_op jit(solution)/shard_map/ppermute | solution.py:33
  81.7 1.9 %collective-permute-start.1 = (bf16[12,176,128]{2,1,0:T(8,128)(2,1)S(1)}, bf16[12,176,128]{2,1,0:T(8,128)(2,1)S(1)}, u32[]{:S(2)}, u32[]{:S(2)}) collective-permute-start(bf16[12,176,128]{2,1,0:T(8,128)(2,1)S(1)} %pad_maximum_fusion), channel_id=1, source_target_pairs={{0,96},{16,48},{32,64},{48,16},{64,32},{80,112},{96,0},{112,80},{1... | collective-permute-start | bytes 1622024 | tf_op jit(solution)/shard_map/ppermute | solution.py:33
  84.4 1.2 broadcast_in_dim.6
  85.6 14.5 %all-to-all-start.3 = ((f32[16,8,128]{2,1,0:T(8,128)}), f32[16,8,128]{2,1,0:T(8,128)}, u32[]{:S(2)}, u32[]{:S(2)}) async-start(f32[16,8,128]{2,1,0:T(8,128)} %broadcast_in_dim.6), calls=%async_computation.3 | async-start | bytes 131072 | tf_op jit(solution)/shard_map/all_to_all | solution.py:46
  100.3 6.7 %collective-permute-start.2 = (bf16[24,176,128]{2,1,0:T(8,128)(2,1)S(1)}, bf16[24,176,128]{2,1,0:T(8,128)(2,1)S(1)}, u32[]{:S(2)}, u32[]{:S(2)}) collective-permute-start(bf16[24,176,128]{2,1,0:T(8,128)(2,1)S(1)} %constant_dynamic-update-slice_fusion.mine_ref), channel_id=1, source_target_pairs={{0,16},{16,0},{32,48},{48,32},{64,80},{80,64},{96,112},{112,96},{1... | collective-permute-start | bytes 3244040 | tf_op jit(solution)/shard_map/ppermute | solution.py:33
  107.1 6.8 %all-to-all-done.3 = f32[16,8,128]{2,1,0:T(8,128)} async-done(((f32[16,8,128]{2,1,0:T(8,128)}), f32[16,8,128]{2,1,0:T(8,128)}, u32[]{:S(2)}, u32[]{:S(2)}) %all-to-all-start.3) | async-done | bytes 65568 | tf_op jit(solution)/shard_map/all_to_all | solution.py:46
  113.9 1.5 slice_reduce_fusion.1
  116.1 28.4 %all_to_all.25 = f32[48,8,128]{2,1,0:T(8,128)S(1)} all-to-all(f32[48,8,128]{2,1,0:T(8,128)S(1)} %broadcast_in_dim.7), channel_id=1, replica_groups=mesh['dp'=48,'tensor'=16] {'dp'}, dimensions={0} | all-to-all | bytes 393216 | tf_op jit(solution)/shard_map/all_to_all | solution.py:46
  147.6 8.9 %apply.1 = bf16[512,128]{1,0:T(8,128)(2,1)} custom-call(s32[1]{0:T(128)} %bitcast.me_ref, bf16[24,176,128]{2,1,0:T(8,128)(2,1)} %copy-done.1, bf16[24,176,128]{2,1,0:T(8,128)(2,1)} %copy-done.4, bf16[512,8192]{1,0:T(8,128)(2,1)} %tokens_hbm.3), custom_call_target="tpu_custom_call" | custom-call | tf_op jit(solution)/shard_map/apply/pallas_call | solution.py:226
  (29 shorter events, 6.7 us)
Async XLA Ops:
  8.2 20.6 %collective-permute-start.3 = (bf16[24,176,128]{2,1,0:T(8,128)(2,1)}, bf16[24,176,128]{2,1,0:T(8,128)(2,1)S(1)}, u32[]{:S(2)}, u32[]{:S(2)}) collective-permute-start(bf16[24,176,128]{2,1,0:T(8,128)(2,1)} %get-tuple-element.12), channel_id=1, source_target_pairs={{0,16},{16,0},{32,48},{48,32},{64,80},{80,64},{96,112},{112,96},{1... | collective-permute-start | bytes 3244040 | tf_op jit(solution)/shard_map/ppermute | solution.py:33
  22.7 23.2 %all-to-all-start = ((bf16[48,32,128]{2,1,0:T(8,128)(2,1)}), bf16[48,32,128]{2,1,0:T(8,128)(2,1)S(1)}, u32[]{:S(2)}, u32[]{:S(2)}) async-start(bf16[48,32,128]{2,1,0:T(8,128)(2,1)} %route.1), calls=%async_computation | async-start | bytes 786432 | tf_op jit(solution)/shard_map/all_to_all | solution.py:247
  28.8 1.0 copy-start.3
  29.8 25.6 %copy-start = (f32[24,176,128]{2,1,0:T(8,128)S(1)}, f32[24,176,128]{2,1,0:T(8,128)}, u32[]{:S(2)}) copy-start(f32[24,176,128]{2,1,0:T(8,128)} %get-tuple-element.11) | copy-start | bytes 6488068
  32.2 23.1 %collective-permute-start.4 = (bf16[12,176,128]{2,1,0:T(8,128)(2,1)}, bf16[12,176,128]{2,1,0:T(8,128)(2,1)S(1)}, u32[]{:S(2)}, u32[]{:S(2)}) collective-permute-start(bf16[12,176,128]{2,1,0:T(8,128)(2,1)} %add_convert_fusion), channel_id=1, source_target_pairs={{0,32},{16,112},{32,0},{48,80},{64,96},{80,48},{96,64},{112,16},{1... | collective-permute-start | bytes 1622024 | tf_op jit(solution)/shard_map/ppermute | solution.py:33
  46.0 0.7 copy-start.2
  48.8 19.8 %all-to-all-start.1 = ((bf16[6,176,128]{2,1,0:T(8,128)(2,1)}), bf16[6,176,128]{2,1,0:T(8,128)(2,1)S(1)}, u32[]{:S(2)}, u32[]{:S(2)}) async-start(bf16[6,176,128]{2,1,0:T(8,128)(2,1)} %get-tuple-element.9), calls=%async_computation.1 | async-start | bytes 540672 | tf_op jit(solution)/shard_map/all_to_all | solution.py:39
  56.4 7.5 %collective-permute-start.5 = (bf16[6,176,128]{2,1,0:T(8,128)(2,1)S(1)}, bf16[6,176,128]{2,1,0:T(8,128)(2,1)S(1)}, u32[]{:S(2)}, u32[]{:S(2)}) collective-permute-start(bf16[6,176,128]{2,1,0:T(8,128)(2,1)S(1)} %add_convert_fusion.2), channel_id=1, source_target_pairs={{0,96},{16,48},{32,64},{48,16},{64,32},{80,112},{96,0},{112,80},{1... | collective-permute-start | bytes 811016 | tf_op jit(solution)/shard_map/ppermute | solution.py:33
  68.6 15.1 %all-to-all-start.2 = ((bf16[6,176,128]{2,1,0:T(8,128)(2,1)}), bf16[6,176,128]{2,1,0:T(8,128)(2,1)S(1)}, u32[]{:S(2)}, u32[]{:S(2)}) async-start(bf16[6,176,128]{2,1,0:T(8,128)(2,1)} %add_convert_fusion.1), calls=%async_computation.2 | async-start | bytes 540672 | tf_op jit(solution)/shard_map/all_to_all | solution.py:39
  73.2 8.4 %collective-permute-start = (bf16[6,176,128]{2,1,0:T(8,128)(2,1)S(1)}, bf16[6,176,128]{2,1,0:T(8,128)(2,1)S(1)}, u32[]{:S(2)}, u32[]{:S(2)}) collective-permute-start(bf16[6,176,128]{2,1,0:T(8,128)(2,1)S(1)} %all-to-all-done.1), channel_id=1, source_target_pairs={{0,32},{16,112},{32,0},{48,80},{64,96},{80,48},{96,64},{112,16},{1... | collective-permute-start | bytes 811016 | tf_op jit(solution)/shard_map/ppermute | solution.py:33
  81.7 18.6 %collective-permute-start.1 = (bf16[12,176,128]{2,1,0:T(8,128)(2,1)S(1)}, bf16[12,176,128]{2,1,0:T(8,128)(2,1)S(1)}, u32[]{:S(2)}, u32[]{:S(2)}) collective-permute-start(bf16[12,176,128]{2,1,0:T(8,128)(2,1)S(1)} %pad_maximum_fusion), channel_id=1, source_target_pairs={{0,96},{16,48},{32,64},{48,16},{64,32},{80,112},{96,0},{112,80},{1... | collective-permute-start | bytes 1622024 | tf_op jit(solution)/shard_map/ppermute | solution.py:33
  85.6 28.3 %all-to-all-start.3 = ((f32[16,8,128]{2,1,0:T(8,128)}), f32[16,8,128]{2,1,0:T(8,128)}, u32[]{:S(2)}, u32[]{:S(2)}) async-start(f32[16,8,128]{2,1,0:T(8,128)} %broadcast_in_dim.6), calls=%async_computation.3 | async-start | bytes 131072 | tf_op jit(solution)/shard_map/all_to_all | solution.py:46
  100.2 45.7 %copy-start.5 = (f32[176,128]{1,0:T(8,128)S(1)}, f32[176,128]{1,0:T(8,128)}, u32[]{:S(2)}) copy-start(f32[176,128]{1,0:T(8,128)} %get-tuple-element.10) | copy-start | bytes 270340
  100.2 45.7 %copy-start.6 = (f32[176,128]{1,0:T(8,128)S(1)}, f32[176,128]{1,0:T(8,128)}, u32[]{:S(2)}) copy-start(f32[176,128]{1,0:T(8,128)} %get-tuple-element.15) | copy-start | bytes 270340
  100.3 46.2 %copy-start.1 = (bf16[24,176,128]{2,1,0:T(8,128)(2,1)}, bf16[24,176,128]{2,1,0:T(8,128)(2,1)S(1)}, u32[]{:S(2)}) copy-start(bf16[24,176,128]{2,1,0:T(8,128)(2,1)S(1)} %constant_dynamic-update-slice_fusion.mine_ref) | copy-start | bytes 3244036
  100.3 46.2 %collective-permute-start.2 = (bf16[24,176,128]{2,1,0:T(8,128)(2,1)S(1)}, bf16[24,176,128]{2,1,0:T(8,128)(2,1)S(1)}, u32[]{:S(2)}, u32[]{:S(2)}) collective-permute-start(bf16[24,176,128]{2,1,0:T(8,128)(2,1)S(1)} %constant_dynamic-update-slice_fusion.mine_ref), channel_id=1, source_target_pairs={{0,16},{16,0},{32,48},{48,32},{64,80},{80,64},{96,112},{112,96},{1... | collective-permute-start | bytes 3244040 | tf_op jit(solution)/shard_map/ppermute | solution.py:33
  146.6 1.0 copy-start.4

commit v2 on v1

--- a/solution.py
+++ b/solution.py
@@ -41,10 +41,8 @@
     )
 
 
-def sum_over(value, axis):
-    copies = jnp.broadcast_to(value, (lax.axis_size(axis), 8, 128))
-    parts = lax.all_to_all(copies, axis, split_axis=0, concat_axis=0, tiled=True)
-    return jnp.sum(parts[:, 0, 0])
+def exchange(copies, axis):
+    return lax.all_to_all(copies, axis, split_axis=0, concat_axis=0, tiled=True)
 
 
 def iota(shape, axis):
@@ -239,6 +237,56 @@
     )(me.reshape(1), mine, other, tokens)
 
 
+def squares_kernel(rows_dev, parts_ref, gradient_ref, copies_ref):
+    gradient = jnp.sum(parts_ref[...].astype(F32), axis=0)
+    gradient_ref[...] = gradient
+    held = jnp.where(iota(gradient.shape, 0) < float(rows_dev), gradient, 0.0)
+    tiles = (held * held).reshape(PAD // 8, 8, 128)
+    copies_ref[...] = jnp.broadcast_to(jnp.sum(tiles, axis=0), copies_ref.shape)
+
+
+def squares_of(parts, rows_dev, count):
+    return pl.pallas_call(
+        functools.partial(squares_kernel, rows_dev),
+        out_shape=(
+            jax.ShapeDtypeStruct((PAD, 128), F32),
+            jax.ShapeDtypeStruct((count, 8, 128), F32),
+        ),
+        name="squares",
+    )(parts)
+
+
+def spread_kernel(parts_ref, copies_ref):
+    copies_ref[...] = jnp.broadcast_to(jnp.sum(parts_ref[...], axis=0), copies_ref.shape)
+
+
+def spread(parts, count):
+    return pl.pallas_call(
+        spread_kernel,
+        out_shape=jax.ShapeDtypeStruct((count, 8, 128), F32),
+        name="spread",
+    )(parts)
+
+
+def update_kernel(parts_ref, gradient_ref, first_ref, second_ref, out_ref):
+    tile = jnp.sum(parts_ref[...], axis=0)
+    squares = jnp.sum(jnp.sum(tile, axis=0, keepdims=True), axis=1, keepdims=True)
+    factor = clip_norm / (jnp.sqrt(squares) + 1e-06)
+    rows = out_ref.shape[0]
+    clipped = gradient_ref[...] * factor
+    moment_one = beta_one * first_ref[...] + (1.0 - beta_one) * clipped
+    moment_two = beta_two * second_ref[...] + (1.0 - beta_two) * clipped * clipped
+    out_ref[...] = (moment_one / (jnp.sqrt(moment_two) + adam_eps))[:rows]
+
+
+def update_of(parts, gradient, first, second, rows_dev):
+    return pl.pallas_call(
+        update_kernel,
+        out_shape=jax.ShapeDtypeStruct((rows_dev, 128), F32),
+        name="update",
+    )(parts, gradient, first, second)
+
+
 def per_device(tokens, cotangent, master, first_moment, second_moment, old_rows):
     rows_dev = master.shape[0]
     me = lax.axis_index("dp")
@@ -256,8 +304,9 @@
     next_x, got_x = lax.optimization_barrier((next_x, got_x))
     last_x = shift(next_x, dx=SECOND)
     sums = keep[18:] + got[18:].astype(F32) + got_x[6:].astype(F32) + last_x.astype(F32)
-    got_z = along_z(sums.astype(BF16))
-    gradient = jnp.sum(got_z.astype(F32), axis=0)[:rows_dev]
+    sums = sums.astype(BF16)
+    got_z = along_z(sums)
+    gradient, copies = squares_of(got_z, rows_dev, lax.axis_size("tensor"))
 
     run = along_z(weight_own)
     west = shift(run, dx=FIRST)
@@ -266,16 +315,12 @@
     mine = jnp.concatenate([pair, rest], axis=0)
     other = shift(mine, dc=1)
 
-    squares = jnp.sum(gradient * gradient)
-    squares = sum_over(squares, "tensor")
-    squares = sum_over(squares, "dp")
+    parts = exchange(copies, "tensor")
+    copies = spread(parts, DP)
+    parts = exchange(copies, "dp")
     keys_values = apply(me, mine, other, tokens, rows_dev)
 
-    factor = clip_norm / (jnp.sqrt(squares) + 1e-06)
-    clipped = gradient * factor
-    moment_one = beta_one * first[:rows_dev] + (1.0 - beta_one) * clipped
-    moment_two = beta_two * second[:rows_dev] + (1.0 - beta_two) * clipped * clipped
-    update = moment_one / (jnp.sqrt(moment_two) + adam_eps)
+    update = update_of(parts, gradient, first, second, rows_dev)
     return (keys_values, update)
 
 

time: 157 us -> 157 us (level)
  blocking collectives: 28.4 us -> 52.4 us
  starting transfers between devices: 61.4 us -> 45.1 us
  waiting for transfers between devices: 30.8 us -> 21.9 us
  Pallas kernels: 20.7 us -> 25.8 us
  other arithmetic: 8.94 us -> 6 us
    all_to_all x1 -> x2, blocking collectives: 28.4 us -> 52.4 us  [exchange(): return lax.all_to_all(copies, axis, split_axis=0, concat_axis=0, tiled=True)]
    all_to_all x1 -> x0, starting transfers between devices: 14.5 us -> none  [sum_over(): lax.all_to_all(copies, axis, split_axis=0, concat_axis=0, tiled=True)]
    ppermute x6, starting transfers between devices: 29.6 us -> 17.8 us  [shift(): return lax.ppermute(value, 'dp', pairs)]
    all_to_all x1, starting transfers between devices: 6.05 us -> 16.4 us  [per_device(): arrived = lax.all_to_all(box, 'dp', split_axis=0, concat_axis=0, tiled=True)]
    all_to_all x1 -> x0, waiting for transfers between devices: 6.85 us -> none  [sum_over(): lax.all_to_all(copies, axis, split_axis=0, concat_axis=0, tiled=True)]
    ppermute x6, waiting for transfers between devices: 11.8 us -> 5.73 us  [shift(): return lax.ppermute(value, 'dp', pairs)]
    all_to_all x2, waiting for transfers between devices: 2.88 us -> 8.73 us  [along_z(): lax.all_to_all(value, 'dp', split_axis=0, concat_axis=0, tiled=True, axis...]
    pallas_call x0 -> x3, Pallas kernels: none -> 5.11 us  [the longest x1 1.91 us: update_of(): pl.pallas_call(update_kernel, out_shape=jax.ShapeDtypeStruct((rows_dev, 1...]
  transfers between devices with their start and end apart: 10 -> 9, of which waited for: 5 -> 5; matrix products, arithmetic and copies ran while one was open for 7% -> 5% of each run, Pallas kernels for 3% -> 9%
where the time goes in v2:
time: 157 us; the launch traced here: 156 us
  blocking collectives  52.4 us (33%)
  starting transfers between devices  45.1 us (29%)
  Pallas kernels  25.8 us (16%)
  waiting for transfers between devices  21.9 us (14%)
  other arithmetic  6 us (4%)
  local copies, waits for them, and re-layouts  4.29 us (3%)
    all_to_all x2, blocking collectives, exchange(): return lax.all_to_all(copies, axis, split_axis=0, concat_axis=0, tiled=True)  52.4 us
    ppermute x6, starting transfers between devices, shift(): return lax.ppermute(value, 'dp', pairs)  17.8 us
    all_to_all x1, starting transfers between devices, per_device(): arrived = lax.all_to_all(box, 'dp', split_axis=0, concat_axis=0, tiled=True)  16.4 us
    all_to_all x2, starting transfers between devices, along_z(): lax.all_to_all(value, 'dp', split_axis=0, concat_axis=0, tiled=True, axis...  10.9 us
    pallas_call x1, Pallas kernels, apply(): pl.pallas_call(functools.partial(apply_kernel, rows_dev), out_shape=jax.S...  8.91 us
    all_to_all x2, waiting for transfers between devices, along_z(): lax.all_to_all(value, 'dp', split_axis=0, concat_axis=0, tiled=True, axis...  8.73 us
    pallas_call x1, Pallas kernels, grad(): pl.pallas_call(functools.partial(grad_kernel, rows_dev), out_shape=(jax.S...  7.49 us
    all_to_all x1, waiting for transfers between devices, per_device(): arrived = lax.all_to_all(box, 'dp', split_axis=0, concat_axis=0, tiled=True)  7.41 us
  transfers between devices with their start and end apart: 9, of which 5 were waited for; matrix products, arithmetic and copies ran while one was open for 5% of the time, Pallas kernels for 9%

profile of v2, /device:TPU:1, one launch (start us, length us, event | category | flops | bytes accessed | tf_op | source)
XLA Modules:
  0.0 156.3 jit_solution(5187006608213260296)
XLA Ops:
  0.6 2.2 %route.1 = bf16[48,32,128]{2,1,0:T(8,128)(2,1)} custom-call(s32[1,171]{1,0:T(1,128)} %bitcast.2, f32[171,128]{1,0:T(8,128)} %master_ref.1, f32[171,128]{1,0:T(8,128)} %first_ref.1, f32[171,128]{1,0:T(8,128)} %second_ref.1), custom_call_target="tpu_custom_call" | custom-call | tf_op jit(solution)/shard_map/route/pallas_call | solution.py:78
  2.8 16.4 %all-to-all-start = ((bf16[48,32,128]{2,1,0:T(8,128)(2,1)}), bf16[48,32,128]{2,1,0:T(8,128)(2,1)S(1)}, u32[]{:S(2)}, u32[]{:S(2)}) async-start(bf16[48,32,128]{2,1,0:T(8,128)(2,1)} %route.1), calls=%async_computation | async-start | bytes 786432 | tf_op jit(solution)/shard_map/all_to_all | solution.py:295
  19.2 7.5 %grad.1 = (bf16[24,176,128]{2,1,0:T(8,128)(2,1)}, f32[24,176,128]{2,1,0:T(8,128)}) custom-call(s32[1]{0:T(128)} %bitcast.me_ref, bf16[512,128]{1,0:T(8,128)(2,1)} %cot_ref.1, bf16[512,8192]{1,0:T(8,128)(2,1)} %tokens_hbm.3), custom_call_target="tpu_custom_call" | custom-call | tf_op jit(solution)/shard_map/grad/pallas_call | solution.py:171
  26.7 2.3 %collective-permute-start.3 = (bf16[24,176,128]{2,1,0:T(8,128)(2,1)}, bf16[24,176,128]{2,1,0:T(8,128)(2,1)S(1)}, u32[]{:S(2)}, u32[]{:S(2)}) collective-permute-start(bf16[24,176,128]{2,1,0:T(8,128)(2,1)} %get-tuple-element.13), channel_id=1, source_target_pairs={{0,16},{16,0},{32,48},{48,32},{64,80},{80,64},{96,112},{112,96},{1... | collective-permute-start | bytes 3244040 | tf_op jit(solution)/shard_map/ppermute | solution.py:33
  29.0 7.4 %all-to-all-done.box_ref = bf16[48,32,128]{2,1,0:T(8,128)(2,1)S(1)} async-done(((bf16[48,32,128]{2,1,0:T(8,128)(2,1)}), bf16[48,32,128]{2,1,0:T(8,128)(2,1)S(1)}, u32[]{:S(2)}, u32[]{:S(2)}) %all-to-all-start) | async-done | bytes 393248 | tf_op jit(solution)/shard_map/all_to_all | solution.py:295
  37.1 2.1 %place.1 = (bf16[6,176,128]{2,1,0:T(8,128)(2,1)}, f32[176,128]{1,0:T(8,128)}, f32[176,128]{1,0:T(8,128)}) custom-call(bf16[48,32,128]{2,1,0:T(8,128)(2,1)} %copy-done.2), custom_call_target="tpu_custom_call" | custom-call | tf_op jit(solution)/shard_map/place/pallas_call | solution.py:106
  39.2 6.5 %all-to-all-start.1 = ((bf16[6,176,128]{2,1,0:T(8,128)(2,1)}), bf16[6,176,128]{2,1,0:T(8,128)(2,1)S(1)}, u32[]{:S(2)}, u32[]{:S(2)}) async-start(bf16[6,176,128]{2,1,0:T(8,128)(2,1)} %get-tuple-element.11), calls=%async_computation.1 | async-start | bytes 540672 | tf_op jit(solution)/shard_map/all_to_all | solution.py:39
  45.8 2.3 %add_convert_fusion = bf16[12,176,128]{2,1,0:T(8,128)(2,1)} fusion(f32[24,176,128]{2,1,0:T(8,128)} %get-tuple-element.12, bf16[24,176,128]{2,1,0:T(8,128)(2,1)S(1)} %collective-permute-done.3), kind=kLoop, calls=%fused_computation | loop fusion | flops 811008 | bytes 2162688 | tf_op jit(solution)/shard_map/convert_element_type | solution.py:300
  48.0 2.2 %collective-permute-start.4 = (bf16[12,176,128]{2,1,0:T(8,128)(2,1)}, bf16[12,176,128]{2,1,0:T(8,128)(2,1)}, u32[]{:S(2)}, u32[]{:S(2)}) collective-permute-start(bf16[12,176,128]{2,1,0:T(8,128)(2,1)} %add_convert_fusion), channel_id=1, source_target_pairs={{0,32},{16,112},{32,0},{48,80},{64,96},{80,48},{96,64},{112,16},{1... | collective-permute-start | bytes 1622024 | tf_op jit(solution)/shard_map/ppermute | solution.py:33
  50.3 8.7 %all-to-all-done.1 = bf16[6,176,128]{2,1,0:T(8,128)(2,1)S(1)} async-done(((bf16[6,176,128]{2,1,0:T(8,128)(2,1)}), bf16[6,176,128]{2,1,0:T(8,128)(2,1)S(1)}, u32[]{:S(2)}, u32[]{:S(2)}) %all-to-all-start.1) | async-done | bytes 270368 | tf_op jit(solution)/shard_map/all_to_all | solution.py:39
  59.0 2.2 %collective-permute-start = (bf16[6,176,128]{2,1,0:T(8,128)(2,1)S(1)}, bf16[6,176,128]{2,1,0:T(8,128)(2,1)S(1)}, u32[]{:S(2)}, u32[]{:S(2)}) collective-permute-start(bf16[6,176,128]{2,1,0:T(8,128)(2,1)S(1)} %all-to-all-done.1), channel_id=1, source_target_pairs={{0,32},{16,112},{32,0},{48,80},{64,96},{80,48},{96,64},{112,16},{1... | collective-permute-start | bytes 811016 | tf_op jit(solution)/shard_map/ppermute | solution.py:33
  62.3 1.9 %collective-permute-start.5 = (bf16[6,176,128]{2,1,0:T(8,128)(2,1)S(1)}, bf16[6,176,128]{2,1,0:T(8,128)(2,1)S(1)}, u32[]{:S(2)}, u32[]{:S(2)}) collective-permute-start(bf16[6,176,128]{2,1,0:T(8,128)(2,1)S(1)} %add_convert_fusion.2), channel_id=1, source_target_pairs={{0,96},{16,48},{32,64},{48,16},{64,32},{80,112},{96,0},{112,80},{1... | collective-permute-start | bytes 811016 | tf_op jit(solution)/shard_map/ppermute | solution.py:33
  64.2 3.2 %collective-permute-done = bf16[6,176,128]{2,1,0:T(8,128)(2,1)S(1)} collective-permute-done((bf16[6,176,128]{2,1,0:T(8,128)(2,1)S(1)}, bf16[6,176,128]{2,1,0:T(8,128)(2,1)S(1)}, u32[]{:S(2)}, u32[]{:S(2)}) %collective-permute-start) | collective-permute-done | bytes 270368 | tf_op jit(solution)/shard_map/ppermute | solution.py:33
  69.0 1.9 %collective-permute-start.1 = (bf16[12,176,128]{2,1,0:T(8,128)(2,1)}, bf16[12,176,128]{2,1,0:T(8,128)(2,1)}, u32[]{:S(2)}, u32[]{:S(2)}) collective-permute-start(bf16[12,176,128]{2,1,0:T(8,128)(2,1)} %pad_maximum_fusion), channel_id=1, source_target_pairs={{0,96},{16,48},{32,64},{48,16},{64,32},{80,112},{96,0},{112,80},{1... | collective-permute-start | bytes 1622024 | tf_op jit(solution)/shard_map/ppermute | solution.py:33
  71.5 1.8 %add_convert_fusion.1 = bf16[6,176,128]{2,1,0:T(8,128)(2,1)} fusion(bf16[6,176,128]{2,1,0:T(8,128)(2,1)S(1)} %collective-permute-done.5, f32[24,176,128]{2,1,0:T(8,128)S(1)} %copy-done, bf16[24,176,128]{2,1,0:T(8,128)(2,1)S(1)} %collective-permute-done.3, bf16[12,176,128]{2,1,0:T(8,128)(2,1)} %collective-permute-done.4), kind=kLoop, calls=%fused_computation.2 | loop fusion | flops 946176 | bytes 1622016 | tf_op jit(solution)/shard_map/convert_element_type | solution.py:307
  73.3 4.4 %all-to-all-start.2 = ((bf16[6,176,128]{2,1,0:T(8,128)(2,1)}), bf16[6,176,128]{2,1,0:T(8,128)(2,1)S(1)}, u32[]{:S(2)}, u32[]{:S(2)}) async-start(bf16[6,176,128]{2,1,0:T(8,128)(2,1)} %add_convert_fusion.1), calls=%async_computation.2 | async-start | bytes 540672 | tf_op jit(solution)/shard_map/all_to_all | solution.py:39
  77.8 1.9 %collective-permute-done.1 = bf16[12,176,128]{2,1,0:T(8,128)(2,1)} collective-permute-done((bf16[12,176,128]{2,1,0:T(8,128)(2,1)}, bf16[12,176,128]{2,1,0:T(8,128)(2,1)}, u32[]{:S(2)}, u32[]{:S(2)}) %collective-permute-start.1) | collective-permute-done | bytes 540704 | tf_op jit(solution)/shard_map/ppermute | solution.py:33
  80.8 7.3 %collective-permute-start.2 = (bf16[24,176,128]{2,1,0:T(8,128)(2,1)S(1)}, bf16[24,176,128]{2,1,0:T(8,128)(2,1)S(1)}, u32[]{:S(2)}, u32[]{:S(2)}) collective-permute-start(bf16[24,176,128]{2,1,0:T(8,128)(2,1)S(1)} %constant_dynamic-update-slice_fusion.mine_ref), channel_id=1, source_target_pairs={{0,16},{16,0},{32,48},{48,32},{64,80},{80,64},{96,112},{112,96},{1... | collective-permute-start | bytes 3244040 | tf_op jit(solution)/shard_map/ppermute | solution.py:33
  88.8 1.7 %squares.1 = (f32[176,128]{1,0:T(8,128)}, f32[16,8,128]{2,1,0:T(8,128)}) custom-call(bf16[6,176,128]{2,1,0:T(8,128)(2,1)} %copy-done.3), custom_call_target="tpu_custom_call" | custom-call | tf_op jit(solution)/shard_map/squares/pallas_call | solution.py:249
  90.5 28.3 %all_to_all.25.parts_ref = f32[16,8,128]{2,1,0:T(8,128)} all-to-all(f32[16,8,128]{2,1,0:T(8,128)} %get-tuple-element.16), channel_id=1, replica_groups=mesh['dp'=48,'tensor'=16] {'tensor'}, dimensions={0} | all-to-all | bytes 131072 | tf_op jit(solution)/shard_map/all_to_all | solution.py:45
  118.8 1.5 spread.1
  120.3 24.2 %all_to_all.26.parts_ref = f32[48,8,128]{2,1,0:T(8,128)} all-to-all(f32[48,8,128]{2,1,0:T(8,128)} %spread.1), channel_id=1, replica_groups=mesh['dp'=48,'tensor'=16] {'dp'}, dimensions={0} | all-to-all | bytes 393216 | tf_op jit(solution)/shard_map/all_to_all | solution.py:45
  144.5 1.9 %update.1 = f32[171,128]{1,0:T(8,128)} custom-call(f32[48,8,128]{2,1,0:T(8,128)} %all_to_all.26.parts_ref, f32[176,128]{1,0:T(8,128)} %get-tuple-element.17.gradient_ref, f32[176,128]{1,0:T(8,128)} %get-tuple-element.18.first_ref, f32[176,128]{1,0:T(8,128)} %get-tuple-element.19.second_ref), custom_call_target="tpu_custom_call" | custom-call | tf_op jit(solution)/shard_map/update/pallas_call | solution.py:283
  147.4 8.9 %apply.1 = bf16[512,128]{1,0:T(8,128)(2,1)} custom-call(s32[1]{0:T(128)} %bitcast.me_ref, bf16[24,176,128]{2,1,0:T(8,128)(2,1)} %copy-done.1, bf16[24,176,128]{2,1,0:T(8,128)(2,1)} %copy-done.6, bf16[512,8192]{1,0:T(8,128)(2,1)} %tokens_hbm.3), custom_call_target="tpu_custom_call" | custom-call | tf_op jit(solution)/shard_map/apply/pallas_call | solution.py:224
  (24 shorter events, 6.9 us)
Async XLA Ops:
  2.8 33.6 %all-to-all-start = ((bf16[48,32,128]{2,1,0:T(8,128)(2,1)}), bf16[48,32,128]{2,1,0:T(8,128)(2,1)S(1)}, u32[]{:S(2)}, u32[]{:S(2)}) async-start(bf16[48,32,128]{2,1,0:T(8,128)(2,1)} %route.1), calls=%async_computation | async-start | bytes 786432 | tf_op jit(solution)/shard_map/all_to_all | solution.py:295
  26.7 19.0 %collective-permute-start.3 = (bf16[24,176,128]{2,1,0:T(8,128)(2,1)}, bf16[24,176,128]{2,1,0:T(8,128)(2,1)S(1)}, u32[]{:S(2)}, u32[]{:S(2)}) collective-permute-start(bf16[24,176,128]{2,1,0:T(8,128)(2,1)} %get-tuple-element.13), channel_id=1, source_target_pairs={{0,16},{16,0},{32,48},{48,32},{64,80},{80,64},{96,112},{112,96},{1... | collective-permute-start | bytes 3244040 | tf_op jit(solution)/shard_map/ppermute | solution.py:33
  36.4 0.7 copy-start.2
  39.2 19.8 %all-to-all-start.1 = ((bf16[6,176,128]{2,1,0:T(8,128)(2,1)}), bf16[6,176,128]{2,1,0:T(8,128)(2,1)S(1)}, u32[]{:S(2)}, u32[]{:S(2)}) async-start(bf16[6,176,128]{2,1,0:T(8,128)(2,1)} %get-tuple-element.11), calls=%async_computation.1 | async-start | bytes 540672 | tf_op jit(solution)/shard_map/all_to_all | solution.py:39
  45.8 15.5 %copy-start = (f32[24,176,128]{2,1,0:T(8,128)S(1)}, f32[24,176,128]{2,1,0:T(8,128)}, u32[]{:S(2)}) copy-start(f32[24,176,128]{2,1,0:T(8,128)} %get-tuple-element.12) | copy-start | bytes 6488068
  48.0 13.2 %collective-permute-start.4 = (bf16[12,176,128]{2,1,0:T(8,128)(2,1)}, bf16[12,176,128]{2,1,0:T(8,128)(2,1)}, u32[]{:S(2)}, u32[]{:S(2)}) collective-permute-start(bf16[12,176,128]{2,1,0:T(8,128)(2,1)} %add_convert_fusion), channel_id=1, source_target_pairs={{0,32},{16,112},{32,0},{48,80},{64,96},{80,48},{96,64},{112,16},{1... | collective-permute-start | bytes 1622024 | tf_op jit(solution)/shard_map/ppermute | solution.py:33
  59.0 8.4 %collective-permute-start = (bf16[6,176,128]{2,1,0:T(8,128)(2,1)S(1)}, bf16[6,176,128]{2,1,0:T(8,128)(2,1)S(1)}, u32[]{:S(2)}, u32[]{:S(2)}) collective-permute-start(bf16[6,176,128]{2,1,0:T(8,128)(2,1)S(1)} %all-to-all-done.1), channel_id=1, source_target_pairs={{0,32},{16,112},{32,0},{48,80},{64,96},{80,48},{96,64},{112,16},{1... | collective-permute-start | bytes 811016 | tf_op jit(solution)/shard_map/ppermute | solution.py:33
  62.3 9.2 %collective-permute-start.5 = (bf16[6,176,128]{2,1,0:T(8,128)(2,1)S(1)}, bf16[6,176,128]{2,1,0:T(8,128)(2,1)S(1)}, u32[]{:S(2)}, u32[]{:S(2)}) collective-permute-start(bf16[6,176,128]{2,1,0:T(8,128)(2,1)S(1)} %add_convert_fusion.2), channel_id=1, source_target_pairs={{0,96},{16,48},{32,64},{48,16},{64,32},{80,112},{96,0},{112,80},{1... | collective-permute-start | bytes 811016 | tf_op jit(solution)/shard_map/ppermute | solution.py:33
  67.4 0.7 copy-start.4
  69.0 10.7 %collective-permute-start.1 = (bf16[12,176,128]{2,1,0:T(8,128)(2,1)}, bf16[12,176,128]{2,1,0:T(8,128)(2,1)}, u32[]{:S(2)}, u32[]{:S(2)}) collective-permute-start(bf16[12,176,128]{2,1,0:T(8,128)(2,1)} %pad_maximum_fusion), channel_id=1, source_target_pairs={{0,96},{16,48},{32,64},{48,16},{64,32},{80,112},{96,0},{112,80},{1... | collective-permute-start | bytes 1622024 | tf_op jit(solution)/shard_map/ppermute | solution.py:33
  73.3 4.4 %copy-start.5 = (bf16[6,176,128]{2,1,0:T(8,128)(2,1)S(1)}, bf16[6,176,128]{2,1,0:T(8,128)(2,1)}, u32[]{:S(2)}) copy-start(bf16[6,176,128]{2,1,0:T(8,128)(2,1)} %copy-done.4) | copy-start | bytes 811012
  73.3 14.8 %all-to-all-start.2 = ((bf16[6,176,128]{2,1,0:T(8,128)(2,1)}), bf16[6,176,128]{2,1,0:T(8,128)(2,1)S(1)}, u32[]{:S(2)}, u32[]{:S(2)}) async-start(bf16[6,176,128]{2,1,0:T(8,128)(2,1)} %add_convert_fusion.1), calls=%async_computation.2 | async-start | bytes 540672 | tf_op jit(solution)/shard_map/all_to_all | solution.py:39
  80.8 65.6 %copy-start.1 = (bf16[24,176,128]{2,1,0:T(8,128)(2,1)}, bf16[24,176,128]{2,1,0:T(8,128)(2,1)S(1)}, u32[]{:S(2)}) copy-start(bf16[24,176,128]{2,1,0:T(8,128)(2,1)S(1)} %constant_dynamic-update-slice_fusion.mine_ref) | copy-start | bytes 3244036
  80.8 65.6 %collective-permute-start.2 = (bf16[24,176,128]{2,1,0:T(8,128)(2,1)S(1)}, bf16[24,176,128]{2,1,0:T(8,128)(2,1)S(1)}, u32[]{:S(2)}, u32[]{:S(2)}) collective-permute-start(bf16[24,176,128]{2,1,0:T(8,128)(2,1)S(1)} %constant_dynamic-update-slice_fusion.mine_ref), channel_id=1, source_target_pairs={{0,16},{16,0},{32,48},{48,32},{64,80},{80,64},{96,112},{112,96},{1... | collective-permute-start | bytes 3244040 | tf_op jit(solution)/shard_map/ppermute | solution.py:33
  88.1 0.7 copy-start.3
  146.4 1.0 copy-start.6

commit v3 on v1

--- a/solution.py
+++ b/solution.py
@@ -23,13 +23,14 @@
 FIRST, SECOND = (1, 3), (3, 1)
 
 
-def shift(value, dx=(0, 0), dc=0):
+def shift(value, da=0, db=0, dx=(0, 0), dc=0):
     pairs = []
     for z in range(NZ):
         for x in range(NX):
             for c in range(NC):
                 source = (z * NX + x) * NC + c
-                pairs.append((source, (z * NX + (x ^ dx[c])) * NC + (c ^ dc)))
+                to_z = (z + 2 * da) % NZ ^ db
+                pairs.append((source, (to_z * NX + (x ^ dx[c])) * NC + (c ^ dc)))
     return lax.ppermute(value, "dp", pairs)
 
 
@@ -97,9 +98,7 @@
     placed = lax.dot_general(
         pick, data, (((0,), (0,)), ((), ())), preferred_element_type=F32
     )
-    weight = placed[:PAD, :128].astype(BF16)
-    for z in range(NZ):
-        weight_ref[z] = weight
+    weight_ref[...] = placed[:PAD, :128].astype(BF16)
     first_ref[...] = placed[:PAD, 128:256]
     second_ref[...] = placed[:PAD, 256:384]
 
@@ -108,7 +107,7 @@
     return pl.pallas_call(
         place_kernel,
         out_shape=(
-            jax.ShapeDtypeStruct((NZ, PAD, 128), BF16),
+            jax.ShapeDtypeStruct((PAD, 128), BF16),
             jax.ShapeDtypeStruct((PAD, 128), F32),
             jax.ShapeDtypeStruct((PAD, 128), F32),
         ),
@@ -198,16 +197,19 @@
     features = tokens_ref.shape[1]
     width = features // BLOCKS
     copies = fetch(tokens_hbm, tokens_ref, sems)
+    my_z = lax.div(me_ref[0], NX * NC)
     my_x, even = lax.rem(lax.div(me_ref[0], NC), NX), lax.rem(me_ref[0], NC) == 0
     total = jnp.zeros(out_ref.shape, F32)
     chip = 0
     for i in range(BLOCKS):
         while chip < DP // NC and 2 * chip * rows_dev < (i + 1) * width:
             z, x = chip // NX, chip % NX
+            back = lax.rem(lax.div(my_z, 2) + 3 - z // 2, 3)
+            back += jnp.where(lax.rem(my_z, 2) == z % 2, 0, 3)
             apart = jnp.bitwise_xor(my_x, x)
             zero, one = pick_of(apart, (0, 6, 18, 12)), pick_of(apart, (0, 12, 18, 6))
-            mine = mine_ref[z + jnp.where(even, zero, one)].astype(F32)
-            other = other_ref[z + jnp.where(even, one, zero)].astype(F32)
+            mine = mine_ref[back + jnp.where(even, zero, one)].astype(F32)
+            other = other_ref[back + jnp.where(even, one, zero)].astype(F32)
             start = 2 * chip * rows_dev
             rows_ref[start : start + PAD, :] = jnp.where(even, mine, other)
             start += rows_dev
@@ -256,10 +258,15 @@
     next_x, got_x = lax.optimization_barrier((next_x, got_x))
     last_x = shift(next_x, dx=SECOND)
     sums = keep[18:] + got[18:].astype(F32) + got_x[6:].astype(F32) + last_x.astype(F32)
-    got_z = along_z(sums.astype(BF16))
+    sums = sums.astype(BF16)
+    got_z = along_z(sums)
     gradient = jnp.sum(got_z.astype(F32), axis=0)[:rows_dev]
 
-    run = along_z(weight_own)
+    one = shift(weight_own, da=1)
+    two = shift(weight_own, da=2)
+    run = jnp.stack([weight_own, one, two])
+    beside = shift(run, db=1)
+    run = jnp.concatenate([run, beside], axis=0)
     west = shift(run, dx=FIRST)
     pair = jnp.concatenate([run, west], axis=0)
     rest = shift(pair, dx=SECOND)

time: 157 us -> 164 us (1.045)
  starting transfers between devices: 61.4 us -> 72.3 us
  waiting for transfers between devices: 30.8 us -> 20.2 us
  local copies, waits for them, and re-layouts: 4.8 us -> 8.94 us
    ppermute x6 -> x9, starting transfers between devices: 29.6 us -> 49.5 us  [shift(): return lax.ppermute(value, 'dp', pairs)]
    all_to_all x1, starting transfers between devices: 14.5 us -> 9.84 us  [sum_over(): lax.all_to_all(copies, axis, split_axis=0, concat_axis=0, tiled=True)]
    all_to_all x2 -> x1, starting transfers between devices: 11.2 us -> 6.92 us  [along_z(): lax.all_to_all(value, 'dp', split_axis=0, concat_axis=0, tiled=True, axis...]
    ppermute x6 -> x9, waiting for transfers between devices: 11.8 us -> 7.65 us  [shift(): return lax.ppermute(value, 'dp', pairs)]
    all_to_all x1, waiting for transfers between devices: 6.85 us -> 3.27 us  [sum_over(): lax.all_to_all(copies, axis, split_axis=0, concat_axis=0, tiled=True)]
    unnamed x16 -> x20, local copies, waits for them, and re-layouts: 2.8 us -> 6.11 us
    all_to_all x2 -> x1, waiting for transfers between devices: 2.88 us -> 0.01 us  [along_z(): lax.all_to_all(value, 'dp', split_axis=0, concat_axis=0, tiled=True, axis...]
  transfers between devices with their start and end apart: 10 -> 12, of which waited for: 5 -> 3; matrix products, arithmetic and copies ran while one was open for 7% -> 9% of each run, Pallas kernels for 3% -> 8%
where the time goes in v3:
time: 164 us; the launch traced here: 163 us
  starting transfers between devices  72.3 us (44%)
  blocking collectives  29.3 us (18%)
  Pallas kernels  20.6 us (13%)
  waiting for transfers between devices  20.2 us (12%)
  other arithmetic  9.66 us (6%)
  local copies, waits for them, and re-layouts  8.94 us (5%)
    ppermute x9, starting transfers between devices, shift(): return lax.ppermute(value, 'dp', pairs)  49.5 us
    all_to_all x1, blocking collectives, sum_over(): lax.all_to_all(copies, axis, split_axis=0, concat_axis=0, tiled=True)  29.3 us
    all_to_all x1, starting transfers between devices, sum_over(): lax.all_to_all(copies, axis, split_axis=0, concat_axis=0, tiled=True)  9.84 us
    all_to_all x1, waiting for transfers between devices, per_device(): arrived = lax.all_to_all(box, 'dp', split_axis=0, concat_axis=0, tiled=True)  9.29 us
    pallas_call x1, Pallas kernels, apply(): pl.pallas_call(functools.partial(apply_kernel, rows_dev), out_shape=jax.S...  8.92 us
    ppermute x9, waiting for transfers between devices, shift(): return lax.ppermute(value, 'dp', pairs)  7.65 us
    pallas_call x1, Pallas kernels, grad(): pl.pallas_call(functools.partial(grad_kernel, rows_dev), out_shape=(jax.S...  7.49 us
    all_to_all x1, starting transfers between devices, along_z(): lax.all_to_all(value, 'dp', split_axis=0, concat_axis=0, tiled=True, axis...  6.92 us
  transfers between devices with their start and end apart: 12, of which 3 were waited for; matrix products, arithmetic and copies ran while one was open for 9% of the time, Pallas kernels for 8%

profile of v3, /device:TPU:1, one launch (start us, length us, event | category | flops | bytes accessed | tf_op | source)
XLA Modules:
  0.0 162.7 jit_solution(7898391019103256807)
XLA Ops:
  0.6 7.5 %grad.1 = (bf16[24,176,128]{2,1,0:T(8,128)(2,1)}, f32[24,176,128]{2,1,0:T(8,128)}) custom-call(s32[1]{0:T(128)} %bitcast.me_ref, bf16[512,128]{1,0:T(8,128)(2,1)} %cot_ref.1, bf16[512,8192]{1,0:T(8,128)(2,1)} %tokens_hbm.3), custom_call_target="tpu_custom_call" | custom-call | tf_op jit(solution)/shard_map/grad/pallas_call | solution.py:172
  8.1 12.4 %collective-permute-start.6 = (bf16[24,176,128]{2,1,0:T(8,128)(2,1)}, bf16[24,176,128]{2,1,0:T(8,128)(2,1)S(1)}, u32[]{:S(2)}, u32[]{:S(2)}) collective-permute-start(bf16[24,176,128]{2,1,0:T(8,128)(2,1)} %get-tuple-element.12), channel_id=1, source_target_pairs={{0,16},{16,0},{32,48},{48,32},{64,80},{80,64},{96,112},{112,96},{1... | collective-permute-start | bytes 3244040 | tf_op jit(solution)/shard_map/ppermute | solution.py:34
  20.5 2.2 %route.1 = bf16[48,32,128]{2,1,0:T(8,128)(2,1)} custom-call(s32[1,171]{1,0:T(1,128)} %bitcast.17, f32[171,128]{1,0:T(8,128)} %master_ref.1, f32[171,128]{1,0:T(8,128)} %first_ref.1, f32[171,128]{1,0:T(8,128)} %second_ref.1), custom_call_target="tpu_custom_call" | custom-call | tf_op jit(solution)/shard_map/route/pallas_call | solution.py:81
  22.7 6.0 %all-to-all-start = ((bf16[48,32,128]{2,1,0:T(8,128)(2,1)}), bf16[48,32,128]{2,1,0:T(8,128)(2,1)S(1)}, u32[]{:S(2)}, u32[]{:S(2)}) async-start(bf16[48,32,128]{2,1,0:T(8,128)(2,1)} %route.1), calls=%async_computation | async-start | bytes 786432 | tf_op jit(solution)/shard_map/all_to_all | solution.py:249
  29.8 2.4 %add_convert_fusion = bf16[12,176,128]{2,1,0:T(8,128)(2,1)} fusion(f32[24,176,128]{2,1,0:T(8,128)} %get-tuple-element.11, bf16[24,176,128]{2,1,0:T(8,128)(2,1)} %copy-done.3), kind=kLoop, calls=%fused_computation | loop fusion | flops 811008 | bytes 2162688 | tf_op jit(solution)/shard_map/convert_element_type | solution.py:254
  32.2 4.5 %collective-permute-start.7 = (bf16[12,176,128]{2,1,0:T(8,128)(2,1)}, bf16[12,176,128]{2,1,0:T(8,128)(2,1)}, u32[]{:S(2)}, u32[]{:S(2)}) collective-permute-start(bf16[12,176,128]{2,1,0:T(8,128)(2,1)} %add_convert_fusion), channel_id=1, source_target_pairs={{0,32},{16,112},{32,0},{48,80},{64,96},{80,48},{96,64},{112,16},{1... | collective-permute-start | bytes 1622024 | tf_op jit(solution)/shard_map/ppermute | solution.py:34
  36.7 9.3 %all-to-all-done.box_ref = bf16[48,32,128]{2,1,0:T(8,128)(2,1)S(1)} async-done(((bf16[48,32,128]{2,1,0:T(8,128)(2,1)}), bf16[48,32,128]{2,1,0:T(8,128)(2,1)S(1)}, u32[]{:S(2)}, u32[]{:S(2)}) %all-to-all-start) | async-done | bytes 393248 | tf_op jit(solution)/shard_map/all_to_all | solution.py:249
  46.7 2.0 %place.1 = (bf16[176,128]{1,0:T(8,128)(2,1)}, f32[176,128]{1,0:T(8,128)}, f32[176,128]{1,0:T(8,128)}) custom-call(bf16[48,32,128]{2,1,0:T(8,128)(2,1)} %copy-done.1), custom_call_target="tpu_custom_call" | custom-call | tf_op jit(solution)/shard_map/place/pallas_call | solution.py:107
  48.7 4.6 %collective-permute-start = (bf16[176,128]{1,0:T(8,128)(2,1)}, bf16[176,128]{1,0:T(8,128)(2,1)S(1)}, u32[]{:S(2)}, u32[]{:S(2)}) collective-permute-start(bf16[176,128]{1,0:T(8,128)(2,1)} %get-tuple-element.9), channel_id=1, source_target_pairs={{0,256},{16,272},{32,288},{48,304},{64,320},{80,336},{96,352},{112... | collective-permute-start | bytes 135176 | tf_op jit(solution)/shard_map/ppermute | solution.py:34
  53.3 4.7 %collective-permute-start.1 = (bf16[176,128]{1,0:T(8,128)(2,1)}, bf16[176,128]{1,0:T(8,128)(2,1)S(1)}, u32[]{:S(2)}, u32[]{:S(2)}) collective-permute-start(bf16[176,128]{1,0:T(8,128)(2,1)} %get-tuple-element.9), channel_id=1, source_target_pairs={{0,512},{16,528},{32,544},{48,560},{64,576},{80,592},{96,608},{112... | collective-permute-start | bytes 135176 | tf_op jit(solution)/shard_map/ppermute | solution.py:34
  58.0 1.4 constant_dynamic-update-slice_fusion.4
  60.3 4.7 %collective-permute-start.2 = (bf16[3,176,128]{2,1,0:T(8,128)(2,1)S(1)}, bf16[3,176,128]{2,1,0:T(8,128)(2,1)S(1)}, u32[]{:S(2)}, u32[]{:S(2)}) collective-permute-start(bf16[3,176,128]{2,1,0:T(8,128)(2,1)S(1)} %pad_maximum_fusion.1), channel_id=1, source_target_pairs={{0,128},{16,144},{32,160},{48,176},{64,192},{80,208},{96,224},{112... | collective-permute-start | bytes 405512 | tf_op jit(solution)/shard_map/ppermute | solution.py:34
  66.7 1.9 %collective-permute-start.8 = (bf16[6,176,128]{2,1,0:T(8,128)(2,1)S(1)}, bf16[6,176,128]{2,1,0:T(8,128)(2,1)S(1)}, u32[]{:S(2)}, u32[]{:S(2)}) collective-permute-start(bf16[6,176,128]{2,1,0:T(8,128)(2,1)S(1)} %add_convert_fusion.2), channel_id=1, source_target_pairs={{0,96},{16,48},{32,64},{48,16},{64,32},{80,112},{96,0},{112,80},{1... | collective-permute-start | bytes 811016 | tf_op jit(solution)/shard_map/ppermute | solution.py:34
  70.0 3.5 %collective-permute-start.3 = (bf16[6,176,128]{2,1,0:T(8,128)(2,1)}, bf16[6,176,128]{2,1,0:T(8,128)(2,1)S(1)}, u32[]{:S(2)}, u32[]{:S(2)}) collective-permute-start(bf16[6,176,128]{2,1,0:T(8,128)(2,1)} %pad_maximum_fusion), channel_id=1, source_target_pairs={{0,32},{16,112},{32,0},{48,80},{64,96},{80,48},{96,64},{112,16},{1... | collective-permute-start | bytes 811016 | tf_op jit(solution)/shard_map/ppermute | solution.py:34
  74.2 1.9 %add_convert_fusion.1 = bf16[6,176,128]{2,1,0:T(8,128)(2,1)} fusion(bf16[6,176,128]{2,1,0:T(8,128)(2,1)S(1)} %collective-permute-done.8, f32[24,176,128]{2,1,0:T(8,128)S(1)} %copy-done, bf16[24,176,128]{2,1,0:T(8,128)(2,1)} %copy-done.3, bf16[12,176,128]{2,1,0:T(8,128)(2,1)} %collective-permute-done.7), kind=kLoop, calls=%fused_computation.2 | loop fusion | flops 946176 | bytes 1622016 | tf_op jit(solution)/shard_map/convert_element_type | solution.py:261
  76.1 6.9 %all-to-all-start.1 = ((bf16[6,176,128]{2,1,0:T(8,128)(2,1)}), bf16[6,176,128]{2,1,0:T(8,128)(2,1)S(1)}, u32[]{:S(2)}, u32[]{:S(2)}) async-start(bf16[6,176,128]{2,1,0:T(8,128)(2,1)} %add_convert_fusion.1), calls=%async_computation.1 | async-start | bytes 540672 | tf_op jit(solution)/shard_map/all_to_all | solution.py:40
  83.8 2.7 %collective-permute-start.4 = (bf16[12,176,128]{2,1,0:T(8,128)(2,1)}, bf16[12,176,128]{2,1,0:T(8,128)(2,1)S(1)}, u32[]{:S(2)}, u32[]{:S(2)}) collective-permute-start(bf16[12,176,128]{2,1,0:T(8,128)(2,1)} %get-tuple-element.16), channel_id=1, source_target_pairs={{0,96},{16,48},{32,64},{48,16},{64,32},{80,112},{96,0},{112,80},{1... | collective-permute-start | bytes 1622024 | tf_op jit(solution)/shard_map/ppermute | solution.py:34
  86.5 7.6 %collective-permute-done.4 = bf16[12,176,128]{2,1,0:T(8,128)(2,1)S(1)} collective-permute-done((bf16[12,176,128]{2,1,0:T(8,128)(2,1)}, bf16[12,176,128]{2,1,0:T(8,128)(2,1)S(1)}, u32[]{:S(2)}, u32[]{:S(2)}) %collective-permute-start.4) | collective-permute-done | bytes 540704 | tf_op jit(solution)/shard_map/ppermute | solution.py:34
  94.3 10.5 %collective-permute-start.5 = (bf16[24,176,128]{2,1,0:T(8,128)(2,1)S(1)}, bf16[24,176,128]{2,1,0:T(8,128)(2,1)S(1)}, u32[]{:S(2)}, u32[]{:S(2)}) collective-permute-start(bf16[24,176,128]{2,1,0:T(8,128)(2,1)S(1)} %constant_dynamic-update-slice_fusion.5.mine_ref), channel_id=1, source_target_pairs={{0,16},{16,0},{32,48},{48,32},{64,80},{80,64},{96,112},{112,96},{1... | collective-permute-start | bytes 3244040 | tf_op jit(solution)/shard_map/ppermute | solution.py:34
  106.1 29.3 %all_to_all.20 = f32[16,8,128]{2,1,0:T(8,128)S(1)} all-to-all(f32[16,8,128]{2,1,0:T(8,128)S(1)} %broadcast_in_dim.6), channel_id=1, replica_groups=mesh['dp'=48,'tensor'=16] {'tensor'}, dimensions={0} | all-to-all | bytes 131072 | tf_op jit(solution)/shard_map/all_to_all | solution.py:47
  136.0 1.3 broadcast_in_dim.7
  137.4 9.8 %all-to-all-start.3 = ((f32[48,8,128]{2,1,0:T(8,128)}), f32[48,8,128]{2,1,0:T(8,128)S(1)}, u32[]{:S(2)}, u32[]{:S(2)}) async-start(f32[48,8,128]{2,1,0:T(8,128)} %broadcast_in_dim.7), calls=%async_computation.3 | async-start | bytes 393216 | tf_op jit(solution)/shard_map/all_to_all | solution.py:47
  148.2 8.9 %apply.1 = bf16[512,128]{1,0:T(8,128)(2,1)} custom-call(s32[1]{0:T(128)} %bitcast.me_ref, bf16[24,176,128]{2,1,0:T(8,128)(2,1)} %copy-done.2, bf16[24,176,128]{2,1,0:T(8,128)(2,1)} %copy-done.4, bf16[512,8192]{1,0:T(8,128)(2,1)} %tokens_hbm.3), custom_call_target="tpu_custom_call" | custom-call | tf_op jit(solution)/shard_map/apply/pallas_call | solution.py:228
  157.2 3.3 %all-to-all-done.3 = f32[48,8,128]{2,1,0:T(8,128)S(1)} async-done(((f32[48,8,128]{2,1,0:T(8,128)}), f32[48,8,128]{2,1,0:T(8,128)S(1)}, u32[]{:S(2)}, u32[]{:S(2)}) %all-to-all-start.3) | async-done | bytes 196640 | tf_op jit(solution)/shard_map/all_to_all | solution.py:47
  (39 shorter events, 11.6 us)
Async XLA Ops:
  8.1 20.6 %collective-permute-start.6 = (bf16[24,176,128]{2,1,0:T(8,128)(2,1)}, bf16[24,176,128]{2,1,0:T(8,128)(2,1)S(1)}, u32[]{:S(2)}, u32[]{:S(2)}) collective-permute-start(bf16[24,176,128]{2,1,0:T(8,128)(2,1)} %get-tuple-element.12), channel_id=1, source_target_pairs={{0,16},{16,0},{32,48},{48,32},{64,80},{80,64},{96,112},{112,96},{1... | collective-permute-start | bytes 3244040 | tf_op jit(solution)/shard_map/ppermute | solution.py:34
  22.7 23.2 %all-to-all-start = ((bf16[48,32,128]{2,1,0:T(8,128)(2,1)}), bf16[48,32,128]{2,1,0:T(8,128)(2,1)S(1)}, u32[]{:S(2)}, u32[]{:S(2)}) async-start(bf16[48,32,128]{2,1,0:T(8,128)(2,1)} %route.1), calls=%async_computation | async-start | bytes 786432 | tf_op jit(solution)/shard_map/all_to_all | solution.py:249
  28.8 1.0 copy-start.3
  29.8 35.8 %copy-start = (f32[24,176,128]{2,1,0:T(8,128)S(1)}, f32[24,176,128]{2,1,0:T(8,128)}, u32[]{:S(2)}) copy-start(f32[24,176,128]{2,1,0:T(8,128)} %get-tuple-element.11) | copy-start | bytes 6488068
  32.2 33.4 %collective-permute-start.7 = (bf16[12,176,128]{2,1,0:T(8,128)(2,1)}, bf16[12,176,128]{2,1,0:T(8,128)(2,1)}, u32[]{:S(2)}, u32[]{:S(2)}) collective-permute-start(bf16[12,176,128]{2,1,0:T(8,128)(2,1)} %add_convert_fusion), channel_id=1, source_target_pairs={{0,32},{16,112},{32,0},{48,80},{64,96},{80,48},{96,64},{112,16},{1... | collective-permute-start | bytes 1622024 | tf_op jit(solution)/shard_map/ppermute | solution.py:34
  46.0 0.8 copy-start.1
  48.7 20.6 %copy-start.5 = (bf16[176,128]{1,0:T(8,128)(2,1)S(1)}, bf16[176,128]{1,0:T(8,128)(2,1)}, u32[]{:S(2)}) copy-start(bf16[176,128]{1,0:T(8,128)(2,1)} %get-tuple-element.9) | copy-start | bytes 135172
  48.7 10.8 %collective-permute-start = (bf16[176,128]{1,0:T(8,128)(2,1)}, bf16[176,128]{1,0:T(8,128)(2,1)S(1)}, u32[]{:S(2)}, u32[]{:S(2)}) collective-permute-start(bf16[176,128]{1,0:T(8,128)(2,1)} %get-tuple-element.9), channel_id=1, source_target_pairs={{0,256},{16,272},{32,288},{48,304},{64,320},{80,336},{96,352},{112... | collective-permute-start | bytes 135176 | tf_op jit(solution)/shard_map/ppermute | solution.py:34
  53.3 6.1 %collective-permute-start.1 = (bf16[176,128]{1,0:T(8,128)(2,1)}, bf16[176,128]{1,0:T(8,128)(2,1)S(1)}, u32[]{:S(2)}, u32[]{:S(2)}) collective-permute-start(bf16[176,128]{1,0:T(8,128)(2,1)} %get-tuple-element.9), channel_id=1, source_target_pairs={{0,512},{16,528},{32,544},{48,560},{64,576},{80,592},{96,608},{112... | collective-permute-start | bytes 135176 | tf_op jit(solution)/shard_map/ppermute | solution.py:34
  60.3 9.0 %collective-permute-start.2 = (bf16[3,176,128]{2,1,0:T(8,128)(2,1)S(1)}, bf16[3,176,128]{2,1,0:T(8,128)(2,1)S(1)}, u32[]{:S(2)}, u32[]{:S(2)}) collective-permute-start(bf16[3,176,128]{2,1,0:T(8,128)(2,1)S(1)} %pad_maximum_fusion.1), channel_id=1, source_target_pairs={{0,128},{16,144},{32,160},{48,176},{64,192},{80,208},{96,224},{112... | collective-permute-start | bytes 405512 | tf_op jit(solution)/shard_map/ppermute | solution.py:34
  66.7 7.5 %collective-permute-start.8 = (bf16[6,176,128]{2,1,0:T(8,128)(2,1)S(1)}, bf16[6,176,128]{2,1,0:T(8,128)(2,1)S(1)}, u32[]{:S(2)}, u32[]{:S(2)}) collective-permute-start(bf16[6,176,128]{2,1,0:T(8,128)(2,1)S(1)} %add_convert_fusion.2), channel_id=1, source_target_pairs={{0,96},{16,48},{32,64},{48,16},{64,32},{80,112},{96,0},{112,80},{1... | collective-permute-start | bytes 811016 | tf_op jit(solution)/shard_map/ppermute | solution.py:34
  70.0 13.0 %collective-permute-start.3 = (bf16[6,176,128]{2,1,0:T(8,128)(2,1)}, bf16[6,176,128]{2,1,0:T(8,128)(2,1)S(1)}, u32[]{:S(2)}, u32[]{:S(2)}) collective-permute-start(bf16[6,176,128]{2,1,0:T(8,128)(2,1)} %pad_maximum_fusion), channel_id=1, source_target_pairs={{0,32},{16,112},{32,0},{48,80},{64,96},{80,48},{96,64},{112,16},{1... | collective-permute-start | bytes 811016 | tf_op jit(solution)/shard_map/ppermute | solution.py:34
  76.1 28.7 %all-to-all-start.1 = ((bf16[6,176,128]{2,1,0:T(8,128)(2,1)}), bf16[6,176,128]{2,1,0:T(8,128)(2,1)S(1)}, u32[]{:S(2)}, u32[]{:S(2)}) async-start(bf16[6,176,128]{2,1,0:T(8,128)(2,1)} %add_convert_fusion.1), calls=%async_computation.1 | async-start | bytes 540672 | tf_op jit(solution)/shard_map/all_to_all | solution.py:40
  83.8 10.4 %collective-permute-start.4 = (bf16[12,176,128]{2,1,0:T(8,128)(2,1)}, bf16[12,176,128]{2,1,0:T(8,128)(2,1)S(1)}, u32[]{:S(2)}, u32[]{:S(2)}) collective-permute-start(bf16[12,176,128]{2,1,0:T(8,128)(2,1)} %get-tuple-element.16), channel_id=1, source_target_pairs={{0,96},{16,48},{32,64},{48,16},{64,32},{80,112},{96,0},{112,80},{1... | collective-permute-start | bytes 1622024 | tf_op jit(solution)/shard_map/ppermute | solution.py:34
  94.3 53.0 %copy-start.2 = (bf16[24,176,128]{2,1,0:T(8,128)(2,1)}, bf16[24,176,128]{2,1,0:T(8,128)(2,1)S(1)}, u32[]{:S(2)}) copy-start(bf16[24,176,128]{2,1,0:T(8,128)(2,1)S(1)} %constant_dynamic-update-slice_fusion.5.mine_ref) | copy-start | bytes 3244036
  94.3 53.0 %collective-permute-start.5 = (bf16[24,176,128]{2,1,0:T(8,128)(2,1)S(1)}, bf16[24,176,128]{2,1,0:T(8,128)(2,1)S(1)}, u32[]{:S(2)}, u32[]{:S(2)}) collective-permute-start(bf16[24,176,128]{2,1,0:T(8,128)(2,1)S(1)} %constant_dynamic-update-slice_fusion.5.mine_ref), channel_id=1, source_target_pairs={{0,16},{16,0},{32,48},{48,32},{64,80},{80,64},{96,112},{112,96},{1... | collective-permute-start | bytes 3244040 | tf_op jit(solution)/shard_map/ppermute | solution.py:34
  137.4 23.1 %all-to-all-start.3 = ((f32[48,8,128]{2,1,0:T(8,128)}), f32[48,8,128]{2,1,0:T(8,128)S(1)}, u32[]{:S(2)}, u32[]{:S(2)}) async-start(f32[48,8,128]{2,1,0:T(8,128)} %broadcast_in_dim.7), calls=%async_computation.3 | async-start | bytes 393216 | tf_op jit(solution)/shard_map/all_to_all | solution.py:47
  147.2 14.7 %copy-start.6 = (f32[176,128]{1,0:T(8,128)S(1)}, f32[176,128]{1,0:T(8,128)}, u32[]{:S(2)}) copy-start(f32[176,128]{1,0:T(8,128)} %get-tuple-element.10) | copy-start | bytes 270340
  147.2 14.7 %copy-start.7 = (f32[176,128]{1,0:T(8,128)S(1)}, f32[176,128]{1,0:T(8,128)}, u32[]{:S(2)}) copy-start(f32[176,128]{1,0:T(8,128)} %get-tuple-element.15) | copy-start | bytes 270340
  147.2 1.0 copy-start.4

commit v4 on v1

--- a/solution.py
+++ b/solution.py
@@ -5,6 +5,7 @@
 from jax import lax
 from jax.experimental import pallas as pl
 from jax.experimental.pallas import tpu as pltpu
+from jax.sharding import Mesh
 from jax.sharding import PartitionSpec as P
 
 beta_one = 0.9
@@ -16,6 +17,7 @@
 NZ, NX, NC = 6, 4, 2
 DP = NZ * NX * NC
 CAP = 8
+ROWS = ("z", "x", "core")
 PAD = 176
 BLOCKS = 8
 
@@ -30,20 +32,16 @@
             for c in range(NC):
                 source = (z * NX + x) * NC + c
                 pairs.append((source, (z * NX + (x ^ dx[c])) * NC + (c ^ dc)))
-    return lax.ppermute(value, "dp", pairs)
+    return lax.ppermute(value, ROWS, pairs)
 
 
 def along_z(value):
-    rest = NX * NC
-    groups = [[z * rest + i for z in range(NZ)] for i in range(rest)]
-    return lax.all_to_all(
-        value, "dp", split_axis=0, concat_axis=0, tiled=True, axis_index_groups=groups
-    )
-
-
-def sum_over(value, axis):
-    copies = jnp.broadcast_to(value, (lax.axis_size(axis), 8, 128))
-    parts = lax.all_to_all(copies, axis, split_axis=0, concat_axis=0, tiled=True)
+    return lax.all_to_all(value, "z", split_axis=0, concat_axis=0, tiled=True)
+
+
+def sum_over(value, axes):
+    copies = jnp.broadcast_to(value, (lax.axis_size(axes), 8, 128))
+    parts = lax.all_to_all(copies, axes, split_axis=0, concat_axis=0, tiled=True)
     return jnp.sum(parts[:, 0, 0])
 
 
@@ -163,7 +161,7 @@
             sent = z + jnp.where(even, one, zero)
             first = whole_ref[2 * chip * rows_dev : 2 * chip * rows_dev + PAD, :]
             second = whole_ref[(2 * chip + 1) * rows_dev : (2 * chip + 1) * rows_dev + PAD, :]
-            keep_ref[kept] = jnp.where(even, first, second)
+            keep_ref[kept] = jnp.where(even, first, second).astype(BF16)
             send_ref[sent] = jnp.where(even, second, first).astype(BF16)
             chip += 1
 
@@ -174,7 +172,7 @@
         functools.partial(grad_kernel, rows_dev),
         out_shape=(
             jax.ShapeDtypeStruct((24, PAD, 128), BF16),
-            jax.ShapeDtypeStruct((24, PAD, 128), F32),
+            jax.ShapeDtypeStruct((24, PAD, 128), BF16),
         ),
         in_specs=[
             pl.BlockSpec(memory_space=pltpu.SMEM),
@@ -193,11 +191,24 @@
 
 
 def apply_kernel(
-    rows_dev, me_ref, mine_ref, other_ref, tokens_hbm, out_ref, tokens_ref, rows_ref, sems
+    rows_dev,
+    me_ref,
+    mine_ref,
+    other_hbm,
+    tokens_hbm,
+    out_ref,
+    other_ref,
+    tokens_ref,
+    rows_ref,
+    sems,
+    row_sem,
 ):
     features = tokens_ref.shape[1]
     width = features // BLOCKS
+    gathered = pltpu.make_async_copy(other_hbm, other_ref, row_sem)
+    gathered.start()
     copies = fetch(tokens_hbm, tokens_ref, sems)
+    gathered.wait()
     my_x, even = lax.rem(lax.div(me_ref[0], NC), NX), lax.rem(me_ref[0], NC) == 0
     total = jnp.zeros(out_ref.shape, F32)
     chip = 0
@@ -227,35 +238,37 @@
         functools.partial(apply_kernel, rows_dev),
         out_shape=jax.ShapeDtypeStruct((tall, 128), BF16),
         in_specs=[pl.BlockSpec(memory_space=pltpu.SMEM)]
-        + [pl.BlockSpec(memory_space=pltpu.VMEM)] * 2
-        + [pl.BlockSpec(memory_space=pltpu.HBM)],
+        + [pl.BlockSpec(memory_space=pltpu.VMEM)]
+        + [pl.BlockSpec(memory_space=pltpu.HBM)] * 2,
         scratch_shapes=[
+            pltpu.VMEM(other.shape, BF16),
             pltpu.VMEM(tokens.shape, BF16),
             pltpu.VMEM((features + 32, 128), F32),
             pltpu.SemaphoreType.DMA((BLOCKS,)),
+            pltpu.SemaphoreType.DMA,
         ],
-        compiler_params=pltpu.CompilerParams(vmem_limit_bytes=60_000_000),
+        compiler_params=pltpu.CompilerParams(vmem_limit_bytes=65_200_000),
         name="apply",
     )(me.reshape(1), mine, other, tokens)
 
 
 def per_device(tokens, cotangent, master, first_moment, second_moment, old_rows):
     rows_dev = master.shape[0]
-    me = lax.axis_index("dp")
+    me = lax.axis_index(ROWS)
 
     box = route(old_rows, master, first_moment, second_moment)
-    arrived = lax.all_to_all(box, "dp", split_axis=0, concat_axis=0, tiled=True)
+    arrived = lax.all_to_all(box, ROWS, split_axis=0, concat_axis=0, tiled=True)
     weight_own, first, second = place(arrived)
 
     send, keep = grad(me, cotangent, tokens, rows_dev)
     got = shift(send, dc=1)
-    next_x = (keep[:12] + got[:12].astype(F32)).astype(BF16)
+    next_x = (keep[:12].astype(F32) + got[:12].astype(F32)).astype(BF16)
     got_x = shift(next_x, dx=FIRST)
-    next_x = keep[12:18] + got[12:18].astype(F32) + got_x[:6].astype(F32)
+    next_x = keep[12:18].astype(F32) + got[12:18].astype(F32) + got_x[:6].astype(F32)
     next_x = next_x.astype(BF16)
     next_x, got_x = lax.optimization_barrier((next_x, got_x))
     last_x = shift(next_x, dx=SECOND)
-    sums = keep[18:] + got[18:].astype(F32) + got_x[6:].astype(F32) + last_x.astype(F32)
+    sums = keep[18:].astype(F32) + got[18:].astype(F32) + got_x[6:].astype(F32) + last_x.astype(F32)
     got_z = along_z(sums.astype(BF16))
     gradient = jnp.sum(got_z.astype(F32), axis=0)[:rows_dev]
 
@@ -267,8 +280,8 @@
     other = shift(mine, dc=1)
 
     squares = jnp.sum(gradient * gradient)
-    squares = sum_over(squares, "tensor")
-    squares = sum_over(squares, "dp")
+    squares = sum_over(squares, ("z", "far"))
+    squares = sum_over(squares, ("x", "core", "y"))
     keys_values = apply(me, mine, other, tokens, rows_dev)
 
     factor = clip_norm / (jnp.sqrt(squares) + 1e-06)
@@ -280,15 +293,17 @@
 
 
 def solution(mesh):
+    rows, columns = ROWS, ("far", "y")
+    fine = Mesh(mesh.devices.reshape(NZ, NX, NC, 2, -1), rows + columns)
     in_specs = (
-        P("dp", None),
-        P("dp", "tensor"),
-        P("dp", "tensor"),
-        P("dp", "tensor"),
-        P("dp", "tensor"),
-        P("dp"),
-    )
-    out_specs = (P("dp", "tensor"), P("dp", "tensor"))
+        P(rows, None),
+        P(rows, columns),
+        P(rows, columns),
+        P(rows, columns),
+        P(rows, columns),
+        P(rows),
+    )
+    out_specs = (P(rows, columns), P(rows, columns))
     return jax.shard_map(
-        per_device, mesh=mesh, in_specs=in_specs, out_specs=out_specs, check_vma=False
-    )
+        per_device, mesh=fine, in_specs=in_specs, out_specs=out_specs, check_vma=False
+    )

time: 157 us -> 149 us (0.949)
  starting transfers between devices: 61.4 us -> 52.6 us
  waiting for transfers between devices: 30.8 us -> 39.1 us
  blocking collectives: 28.4 us -> 24.3 us
  other arithmetic: 8.94 us -> 5.76 us
  local copies, waits for them, and re-layouts: 4.8 us -> 2.79 us
    all_to_all x4, waiting for transfers between devices: 19 us -> 38.2 us  [the longest x2 20.5 us: along_z(): return lax.all_to_all(value, 'z', split_axis=0, concat_axis=0, tiled=True)]
    ppermute x6, waiting for transfers between devices: 11.8 us -> 0.94 us  [shift(): return lax.ppermute(value, ROWS, pairs)]
    all_to_all x4, starting transfers between devices: 31.8 us -> 25.6 us  [the longest x2 9.97 us: along_z(): return lax.all_to_all(value, 'z', split_axis=0, concat_axis=0, tiled=True)]
    all_to_all x1, blocking collectives: 28.4 us -> 24.3 us  [sum_over(): lax.all_to_all(copies, axes, split_axis=0, concat_axis=0, tiled=True)]
    ppermute x6, starting transfers between devices: 29.6 us -> 27 us  [shift(): return lax.ppermute(value, ROWS, pairs)]
    convert_element_type x1, other arithmetic: 2.43 us -> 0.14 us  [per_device(): next_x = (keep[:12].astype(F32) + got[:12].astype(F32)).astype(BF16)]
    unnamed x16 -> x12, local copies, waits for them, and re-layouts: 2.8 us -> 0.82 us
    pallas_call x1, Pallas kernels: 8.91 us -> 10.6 us  [apply(): pl.pallas_call(functools.partial(apply_kernel, rows_dev), out_shape=jax.S...]
  transfers between devices with their start and end apart: 10 -> 10, of which waited for: 5 -> 5; matrix products, arithmetic and copies ran while one was open for 7% -> 5% of each run, Pallas kernels for 3% -> 3%
where the time goes in v4:
time: 149 us; the launch traced here: 148 us
  starting transfers between devices  52.6 us (35%)
  waiting for transfers between devices  39.1 us (26%)
  blocking collectives  24.3 us (16%)
  Pallas kernels  22.1 us (15%)
  other arithmetic  5.76 us (4%)
  local copies, waits for them, and re-layouts  2.79 us (2%)
  between operations  1.57 us (1%)
    ppermute x6, starting transfers between devices, shift(): return lax.ppermute(value, ROWS, pairs)  27 us
    all_to_all x1, blocking collectives, sum_over(): lax.all_to_all(copies, axes, split_axis=0, concat_axis=0, tiled=True)  24.3 us
    all_to_all x2, waiting for transfers between devices, along_z(): return lax.all_to_all(value, 'z', split_axis=0, concat_axis=0, tiled=True)  20.5 us
    all_to_all x1, waiting for transfers between devices, per_device(): arrived = lax.all_to_all(box, ROWS, split_axis=0, concat_axis=0, tiled=True)  12.5 us
    pallas_call x1, Pallas kernels, apply(): pl.pallas_call(functools.partial(apply_kernel, rows_dev), out_shape=jax.S...  10.6 us
    all_to_all x2, starting transfers between devices, along_z(): return lax.all_to_all(value, 'z', split_axis=0, concat_axis=0, tiled=True)  9.97 us
    all_to_all x1, starting transfers between devices, sum_over(): lax.all_to_all(copies, axes, split_axis=0, concat_axis=0, tiled=True)  9.56 us
    pallas_call x1, Pallas kernels, grad(): pl.pallas_call(functools.partial(grad_kernel, rows_dev), out_shape=(jax.S...  7.18 us
  transfers between devices with their start and end apart: 10, of which 5 were waited for; matrix products, arithmetic and copies ran while one was open for 5% of the time, Pallas kernels for 3%

profile of v4, /device:TPU:1, one launch (start us, length us, event | category | flops | bytes accessed | tf_op | source)
XLA Modules:
  0.0 148.1 jit_solution(14404108176610727307)
XLA Ops:
  0.6 7.2 %grad.1 = (bf16[24,176,128]{2,1,0:T(8,128)(2,1)}, bf16[24,176,128]{2,1,0:T(8,128)(2,1)}) custom-call(s32[1]{0:T(128)} %bitcast.me_ref, bf16[512,128]{1,0:T(8,128)(2,1)} %cot_ref.1, bf16[512,8192]{1,0:T(8,128)(2,1)} %tokens_hbm.3), custom_call_target="tpu_custom_call" | custom-call | tf_op jit(solution)/shard_map/grad/pallas_call | solution.py:171
  7.8 12.5 %collective-permute-start.3 = (bf16[24,176,128]{2,1,0:T(8,128)(2,1)}, bf16[24,176,128]{2,1,0:T(8,128)(2,1)S(1)}, u32[]{:S(2)}, u32[]{:S(2)}) collective-permute-start(bf16[24,176,128]{2,1,0:T(8,128)(2,1)} %get-tuple-element.12), channel_id=1, source_target_pairs={{0,16},{16,0},{32,48},{48,32},{64,80},{80,64},{96,112},{112,96},{1... | collective-permute-start | bytes 3244040 | tf_op jit(solution)/shard_map/ppermute | solution.py:35
  20.4 2.2 %route.1 = bf16[48,32,128]{2,1,0:T(8,128)(2,1)} custom-call(s32[1,171]{1,0:T(1,128)} %bitcast.2, f32[171,128]{1,0:T(8,128)} %master_ref.1, f32[171,128]{1,0:T(8,128)} %first_ref.1, f32[171,128]{1,0:T(8,128)} %second_ref.1), custom_call_target="tpu_custom_call" | custom-call | tf_op jit(solution)/shard_map/route/pallas_call | solution.py:78
  22.5 6.0 %all-to-all-start = ((bf16[48,32,128]{2,1,0:T(8,128)(2,1)}), bf16[48,32,128]{2,1,0:T(8,128)(2,1)S(1)}, u32[]{:S(2)}, u32[]{:S(2)}) async-start(bf16[48,32,128]{2,1,0:T(8,128)(2,1)} %route.1), calls=%async_computation | async-start | bytes 786432 | tf_op jit(solution)/shard_map/all_to_all | solution.py:260
  28.8 4.5 %collective-permute-start.4 = (bf16[12,176,128]{2,1,0:T(8,128)(2,1)S(1)}, bf16[12,176,128]{2,1,0:T(8,128)(2,1)}, u32[]{:S(2)}, u32[]{:S(2)}) collective-permute-start(bf16[12,176,128]{2,1,0:T(8,128)(2,1)S(1)} %add_convert_fusion), channel_id=1, source_target_pairs={{0,32},{16,112},{32,0},{48,80},{64,96},{80,48},{96,64},{112,16},{1... | collective-permute-start | bytes 1622024 | tf_op jit(solution)/shard_map/ppermute | solution.py:35
  33.2 12.5 %all-to-all-done.box_ref = bf16[48,32,128]{2,1,0:T(8,128)(2,1)S(1)} async-done(((bf16[48,32,128]{2,1,0:T(8,128)(2,1)}), bf16[48,32,128]{2,1,0:T(8,128)(2,1)S(1)}, u32[]{:S(2)}, u32[]{:S(2)}) %all-to-all-start) | async-done | bytes 393248 | tf_op jit(solution)/shard_map/all_to_all | solution.py:260
  45.8 0.7 copy-done.1
  46.5 2.1 %place.1 = (bf16[6,176,128]{2,1,0:T(8,128)(2,1)}, f32[176,128]{1,0:T(8,128)}, f32[176,128]{1,0:T(8,128)}) custom-call(bf16[48,32,128]{2,1,0:T(8,128)(2,1)} %copy-done.1), custom_call_target="tpu_custom_call" | custom-call | tf_op jit(solution)/shard_map/place/pallas_call | solution.py:106
  48.6 6.5 %all-to-all-start.1 = ((bf16[6,176,128]{2,1,0:T(8,128)(2,1)}), bf16[6,176,128]{2,1,0:T(8,128)(2,1)S(1)}, u32[]{:S(2)}, u32[]{:S(2)}) async-start(bf16[6,176,128]{2,1,0:T(8,128)(2,1)} %get-tuple-element.9), calls=%async_computation.1 | async-start | bytes 540672 | tf_op jit(solution)/shard_map/all_to_all | solution.py:39
  55.1 1.1 add_convert_fusion.2
  56.2 1.9 %collective-permute-start.5 = (bf16[6,176,128]{2,1,0:T(8,128)(2,1)S(1)}, bf16[6,176,128]{2,1,0:T(8,128)(2,1)S(1)}, u32[]{:S(2)}, u32[]{:S(2)}) collective-permute-start(bf16[6,176,128]{2,1,0:T(8,128)(2,1)S(1)} %add_convert_fusion.2), channel_id=1, source_target_pairs={{0,96},{16,48},{32,64},{48,16},{64,32},{80,112},{96,0},{112,80},{1... | collective-permute-start | bytes 811016 | tf_op jit(solution)/shard_map/ppermute | solution.py:35
  58.1 10.3 %all-to-all-done.1 = bf16[6,176,128]{2,1,0:T(8,128)(2,1)S(1)} async-done(((bf16[6,176,128]{2,1,0:T(8,128)(2,1)}), bf16[6,176,128]{2,1,0:T(8,128)(2,1)S(1)}, u32[]{:S(2)}, u32[]{:S(2)}) %all-to-all-start.1) | async-done | bytes 270368 | tf_op jit(solution)/shard_map/all_to_all | solution.py:39
  68.4 2.2 %collective-permute-start = (bf16[6,176,128]{2,1,0:T(8,128)(2,1)S(1)}, bf16[6,176,128]{2,1,0:T(8,128)(2,1)S(1)}, u32[]{:S(2)}, u32[]{:S(2)}) collective-permute-start(bf16[6,176,128]{2,1,0:T(8,128)(2,1)S(1)} %all-to-all-done.1), channel_id=1, source_target_pairs={{0,32},{16,112},{32,0},{48,80},{64,96},{80,48},{96,64},{112,16},{1... | collective-permute-start | bytes 811016 | tf_op jit(solution)/shard_map/ppermute | solution.py:35
  70.6 1.8 %add_convert_fusion.1 = bf16[6,176,128]{2,1,0:T(8,128)(2,1)} fusion(bf16[6,176,128]{2,1,0:T(8,128)(2,1)S(1)} %collective-permute-done.5, bf16[24,176,128]{2,1,0:T(8,128)(2,1)S(1)} %collective-permute-done.3, bf16[12,176,128]{2,1,0:T(8,128)(2,1)} %collective-permute-done.4, bf16[24,176,128]{2,1,0:T(8,128)(2,1)S(1)} %copy-done.2), kind=kLoop, calls=%fused_computation.3 | loop fusion | flops 1081344 | bytes 1351680 | tf_op jit(solution)/shard_map/convert_element_type | solution.py:272
  72.4 3.4 %all-to-all-start.2 = ((bf16[6,176,128]{2,1,0:T(8,128)(2,1)}), bf16[6,176,128]{2,1,0:T(8,128)(2,1)S(1)}, u32[]{:S(2)}, u32[]{:S(2)}) async-start(bf16[6,176,128]{2,1,0:T(8,128)(2,1)} %add_convert_fusion.1), calls=%async_computation.2 | async-start | bytes 540672 | tf_op jit(solution)/shard_map/all_to_all | solution.py:39
  75.9 0.9 collective-permute-done
  76.8 1.9 %collective-permute-start.1 = (bf16[12,176,128]{2,1,0:T(8,128)(2,1)S(1)}, bf16[12,176,128]{2,1,0:T(8,128)(2,1)S(1)}, u32[]{:S(2)}, u32[]{:S(2)}) collective-permute-start(bf16[12,176,128]{2,1,0:T(8,128)(2,1)S(1)} %pad_maximum_fusion), channel_id=1, source_target_pairs={{0,96},{16,48},{32,64},{48,16},{64,32},{80,112},{96,0},{112,80},{1... | collective-permute-start | bytes 1622024 | tf_op jit(solution)/shard_map/ppermute | solution.py:35
  78.8 10.3 %all-to-all-done.2 = bf16[6,176,128]{2,1,0:T(8,128)(2,1)S(1)} async-done(((bf16[6,176,128]{2,1,0:T(8,128)(2,1)}), bf16[6,176,128]{2,1,0:T(8,128)(2,1)S(1)}, u32[]{:S(2)}, u32[]{:S(2)}) %all-to-all-start.2) | async-done | bytes 270368 | tf_op jit(solution)/shard_map/all_to_all | solution.py:39
  89.8 1.2 broadcast_in_dim.6
  91.1 9.6 %all-to-all-start.3 = ((f32[12,8,128]{2,1,0:T(8,128)}), f32[12,8,128]{2,1,0:T(8,128)S(1)}, u32[]{:S(2)}, u32[]{:S(2)}) async-start(f32[12,8,128]{2,1,0:T(8,128)} %broadcast_in_dim.6), calls=%async_computation.3 | async-start | bytes 98304 | tf_op jit(solution)/shard_map/all_to_all | solution.py:44
  100.7 3.9 %collective-permute-start.2 = (bf16[24,176,128]{2,1,0:T(8,128)(2,1)S(1)}, bf16[24,176,128]{2,1,0:T(8,128)(2,1)}, u32[]{:S(2)}, u32[]{:S(2)}) collective-permute-start(bf16[24,176,128]{2,1,0:T(8,128)(2,1)S(1)} %constant_dynamic-update-slice_fusion.mine_ref), channel_id=1, source_target_pairs={{0,16},{16,0},{32,48},{48,32},{64,80},{80,64},{96,112},{112,96},{1... | collective-permute-start | bytes 3244040 | tf_op jit(solution)/shard_map/ppermute | solution.py:35
  104.7 5.1 %all-to-all-done.3 = f32[12,8,128]{2,1,0:T(8,128)S(1)} async-done(((f32[12,8,128]{2,1,0:T(8,128)}), f32[12,8,128]{2,1,0:T(8,128)S(1)}, u32[]{:S(2)}, u32[]{:S(2)}) %all-to-all-start.3) | async-done | bytes 49184 | tf_op jit(solution)/shard_map/all_to_all | solution.py:44
  111.1 24.3 %all_to_all.25 = f32[64,8,128]{2,1,0:T(8,128)S(1)} all-to-all(f32[64,8,128]{2,1,0:T(8,128)S(1)} %broadcast_in_dim.7), channel_id=1, replica_groups=mesh['z'=6,'x'=4,'core'=2,'far'=2,'y'=8] {'x','core','y'}, dimensions={0} | all-to-all | bytes 524288 | tf_op jit(solution)/shard_map/all_to_all | solution.py:44
  137.5 10.6 %apply.1 = bf16[512,128]{1,0:T(8,128)(2,1)} custom-call(s32[1]{0:T(128)} %bitcast.me_ref, bf16[24,176,128]{2,1,0:T(8,128)(2,1)} %copy-done, bf16[24,176,128]{2,1,0:T(8,128)(2,1)} %collective-permute-done.2.other_hbm, bf16[512,8192]{1,0:T(8,128)(2,1)} %tokens_hbm.3), custom_call_target="tpu_custom_call" | custom-call | tf_op jit(solution)/shard_map/apply/pallas_call | solution.py:237
  (25 shorter events, 3.7 us)
Async XLA Ops:
  7.8 20.8 %copy-start.2 = (bf16[24,176,128]{2,1,0:T(8,128)(2,1)S(1)}, bf16[24,176,128]{2,1,0:T(8,128)(2,1)}, u32[]{:S(2)}) copy-start(bf16[24,176,128]{2,1,0:T(8,128)(2,1)} %get-tuple-element.11) | copy-start | bytes 3244036
  7.8 20.8 %collective-permute-start.3 = (bf16[24,176,128]{2,1,0:T(8,128)(2,1)}, bf16[24,176,128]{2,1,0:T(8,128)(2,1)S(1)}, u32[]{:S(2)}, u32[]{:S(2)}) collective-permute-start(bf16[24,176,128]{2,1,0:T(8,128)(2,1)} %get-tuple-element.12), channel_id=1, source_target_pairs={{0,16},{16,0},{32,48},{48,32},{64,80},{80,64},{96,112},{112,96},{1... | collective-permute-start | bytes 3244040 | tf_op jit(solution)/shard_map/ppermute | solution.py:35
  22.5 23.2 %all-to-all-start = ((bf16[48,32,128]{2,1,0:T(8,128)(2,1)}), bf16[48,32,128]{2,1,0:T(8,128)(2,1)S(1)}, u32[]{:S(2)}, u32[]{:S(2)}) async-start(bf16[48,32,128]{2,1,0:T(8,128)(2,1)} %route.1), calls=%async_computation | async-start | bytes 786432 | tf_op jit(solution)/shard_map/all_to_all | solution.py:260
  28.8 26.4 %collective-permute-start.4 = (bf16[12,176,128]{2,1,0:T(8,128)(2,1)S(1)}, bf16[12,176,128]{2,1,0:T(8,128)(2,1)}, u32[]{:S(2)}, u32[]{:S(2)}) collective-permute-start(bf16[12,176,128]{2,1,0:T(8,128)(2,1)S(1)} %add_convert_fusion), channel_id=1, source_target_pairs={{0,32},{16,112},{32,0},{48,80},{64,96},{80,48},{96,64},{112,16},{1... | collective-permute-start | bytes 1622024 | tf_op jit(solution)/shard_map/ppermute | solution.py:35
  45.8 0.7 copy-start.1
  48.6 19.8 %all-to-all-start.1 = ((bf16[6,176,128]{2,1,0:T(8,128)(2,1)}), bf16[6,176,128]{2,1,0:T(8,128)(2,1)S(1)}, u32[]{:S(2)}, u32[]{:S(2)}) async-start(bf16[6,176,128]{2,1,0:T(8,128)(2,1)} %get-tuple-element.9), calls=%async_computation.1 | async-start | bytes 540672 | tf_op jit(solution)/shard_map/all_to_all | solution.py:39
  56.2 14.4 %collective-permute-start.5 = (bf16[6,176,128]{2,1,0:T(8,128)(2,1)S(1)}, bf16[6,176,128]{2,1,0:T(8,128)(2,1)S(1)}, u32[]{:S(2)}, u32[]{:S(2)}) collective-permute-start(bf16[6,176,128]{2,1,0:T(8,128)(2,1)S(1)} %add_convert_fusion.2), channel_id=1, source_target_pairs={{0,96},{16,48},{32,64},{48,16},{64,32},{80,112},{96,0},{112,80},{1... | collective-permute-start | bytes 811016 | tf_op jit(solution)/shard_map/ppermute | solution.py:35
  68.4 8.4 %collective-permute-start = (bf16[6,176,128]{2,1,0:T(8,128)(2,1)S(1)}, bf16[6,176,128]{2,1,0:T(8,128)(2,1)S(1)}, u32[]{:S(2)}, u32[]{:S(2)}) collective-permute-start(bf16[6,176,128]{2,1,0:T(8,128)(2,1)S(1)} %all-to-all-done.1), channel_id=1, source_target_pairs={{0,32},{16,112},{32,0},{48,80},{64,96},{80,48},{96,64},{112,16},{1... | collective-permute-start | bytes 811016 | tf_op jit(solution)/shard_map/ppermute | solution.py:35
  72.4 16.7 %all-to-all-start.2 = ((bf16[6,176,128]{2,1,0:T(8,128)(2,1)}), bf16[6,176,128]{2,1,0:T(8,128)(2,1)S(1)}, u32[]{:S(2)}, u32[]{:S(2)}) async-start(bf16[6,176,128]{2,1,0:T(8,128)(2,1)} %add_convert_fusion.1), calls=%async_computation.2 | async-start | bytes 540672 | tf_op jit(solution)/shard_map/all_to_all | solution.py:39
  76.8 23.8 %collective-permute-start.1 = (bf16[12,176,128]{2,1,0:T(8,128)(2,1)S(1)}, bf16[12,176,128]{2,1,0:T(8,128)(2,1)S(1)}, u32[]{:S(2)}, u32[]{:S(2)}) collective-permute-start(bf16[12,176,128]{2,1,0:T(8,128)(2,1)S(1)} %pad_maximum_fusion), channel_id=1, source_target_pairs={{0,96},{16,48},{32,64},{48,16},{64,32},{80,112},{96,0},{112,80},{1... | collective-permute-start | bytes 1622024 | tf_op jit(solution)/shard_map/ppermute | solution.py:35
  89.2 47.6 %copy-start.3 = (f32[176,128]{1,0:T(8,128)S(1)}, f32[176,128]{1,0:T(8,128)}, u32[]{:S(2)}) copy-start(f32[176,128]{1,0:T(8,128)} %get-tuple-element.10) | copy-start | bytes 270340
  89.2 47.6 %copy-start.4 = (f32[176,128]{1,0:T(8,128)S(1)}, f32[176,128]{1,0:T(8,128)}, u32[]{:S(2)}) copy-start(f32[176,128]{1,0:T(8,128)} %get-tuple-element.15) | copy-start | bytes 270340
  91.1 18.7 %all-to-all-start.3 = ((f32[12,8,128]{2,1,0:T(8,128)}), f32[12,8,128]{2,1,0:T(8,128)S(1)}, u32[]{:S(2)}, u32[]{:S(2)}) async-start(f32[12,8,128]{2,1,0:T(8,128)} %broadcast_in_dim.6), calls=%async_computation.3 | async-start | bytes 98304 | tf_op jit(solution)/shard_map/all_to_all | solution.py:44
  100.7 36.8 %copy-start = (bf16[24,176,128]{2,1,0:T(8,128)(2,1)}, bf16[24,176,128]{2,1,0:T(8,128)(2,1)S(1)}, u32[]{:S(2)}) copy-start(bf16[24,176,128]{2,1,0:T(8,128)(2,1)S(1)} %constant_dynamic-update-slice_fusion.mine_ref) | copy-start | bytes 3244036
  100.7 36.8 %collective-permute-start.2 = (bf16[24,176,128]{2,1,0:T(8,128)(2,1)S(1)}, bf16[24,176,128]{2,1,0:T(8,128)(2,1)}, u32[]{:S(2)}, u32[]{:S(2)}) collective-permute-start(bf16[24,176,128]{2,1,0:T(8,128)(2,1)S(1)} %constant_dynamic-update-slice_fusion.mine_ref), channel_id=1, source_target_pairs={{0,16},{16,0},{32,48},{48,32},{64,80},{80,64},{96,112},{112,96},{1... | collective-permute-start | bytes 3244040 | tf_op jit(solution)/shard_map/ppermute | solution.py:35

commit v5 on v4

--- a/solution.py
+++ b/solution.py
@@ -20,6 +20,7 @@
 ROWS = ("z", "x", "core")
 PAD = 176
 BLOCKS = 8
+AHEAD = 3
 
 
 FIRST, SECOND = (1, 3), (3, 1)
@@ -131,9 +132,15 @@
         )
         for i in range(BLOCKS)
     ]
-    for copy in copies:
+    for copy in copies[:AHEAD]:
         copy.start()
     return copies
+
+
+def take(copies, index):
+    copies[index].wait()
+    if index + AHEAD < len(copies):
+        copies[index + AHEAD].start()
 
 
 def grad_kernel(
@@ -147,7 +154,7 @@
     turned = cot_ref[...].T
     chip = 0
     for i in range(BLOCKS):
-        copies[i].wait()
+        take(copies, i)
         across = jnp.dot(
             turned, tokens_ref[:, i * width : i * width + width], preferred_element_type=F32
         )
@@ -201,31 +208,39 @@
     tokens_ref,
     rows_ref,
     sems,
-    row_sem,
+    row_sems,
 ):
     features = tokens_ref.shape[1]
     width = features // BLOCKS
-    gathered = pltpu.make_async_copy(other_hbm, other_ref, row_sem)
-    gathered.start()
+    my_x, even = lax.rem(lax.div(me_ref[0], NC), NX), lax.rem(me_ref[0], NC) == 0
+    places, gathered = [], []
+    for chip in range(DP // NC):
+        z, x = chip // NX, chip % NX
+        apart = jnp.bitwise_xor(my_x, x)
+        zero, one = pick_of(apart, (0, 6, 18, 12)), pick_of(apart, (0, 12, 18, 6))
+        places.append(z + jnp.where(even, zero, one))
+        gathered.append(
+            pltpu.make_async_copy(
+                other_hbm.at[z + jnp.where(even, one, zero)],
+                other_ref.at[chip],
+                row_sems.at[chip],
+            )
+        )
+        gathered[chip].start()
     copies = fetch(tokens_hbm, tokens_ref, sems)
-    gathered.wait()
-    my_x, even = lax.rem(lax.div(me_ref[0], NC), NX), lax.rem(me_ref[0], NC) == 0
     total = jnp.zeros(out_ref.shape, F32)
     chip = 0
     for i in range(BLOCKS):
         while chip < DP // NC and 2 * chip * rows_dev < (i + 1) * width:
-            z, x = chip // NX, chip % NX
-            apart = jnp.bitwise_xor(my_x, x)
-            zero, one = pick_of(apart, (0, 6, 18, 12)), pick_of(apart, (0, 12, 18, 6))
-            mine = mine_ref[z + jnp.where(even, zero, one)].astype(F32)
-            other = other_ref[z + jnp.where(even, one, zero)].astype(F32)
+            gathered[chip].wait()
+            mine, other = mine_ref[places[chip]].astype(F32), other_ref[chip].astype(F32)
             start = 2 * chip * rows_dev
             rows_ref[start : start + PAD, :] = jnp.where(even, mine, other)
             start += rows_dev
             rows_ref[start : start + PAD, :] = jnp.where(even, other, mine)
             chip += 1
         block = slice(i * width, i * width + width)
-        copies[i].wait()
+        take(copies, i)
         total += jnp.dot(
             tokens_ref[:, block], rows_ref[block, :].astype(BF16), preferred_element_type=F32
         )
@@ -245,7 +260,7 @@
             pltpu.VMEM(tokens.shape, BF16),
             pltpu.VMEM((features + 32, 128), F32),
             pltpu.SemaphoreType.DMA((BLOCKS,)),
-            pltpu.SemaphoreType.DMA,
+            pltpu.SemaphoreType.DMA((DP // NC,)),
         ],
         compiler_params=pltpu.CompilerParams(vmem_limit_bytes=65_200_000),
         name="apply",

time: 149 us -> 148 us (level)
  no operation moved by 1% of the time
where the time goes in v5:
time: 148 us; the launch traced here: 147 us
  starting transfers between devices  52.6 us (36%)
  waiting for transfers between devices  39.1 us (26%)
  blocking collectives  24.3 us (16%)
  Pallas kernels  20.8 us (14%)
  other arithmetic  5.76 us (4%)
  local copies, waits for them, and re-layouts  2.79 us (2%)
  between operations  1.57 us (1%)
    ppermute x6, starting transfers between devices, shift(): return lax.ppermute(value, ROWS, pairs)  27 us
    all_to_all x1, blocking collectives, sum_over(): lax.all_to_all(copies, axes, split_axis=0, concat_axis=0, tiled=True)  24.3 us
    all_to_all x2, waiting for transfers between devices, along_z(): return lax.all_to_all(value, 'z', split_axis=0, concat_axis=0, tiled=True)  20.5 us
    all_to_all x1, waiting for transfers between devices, per_device(): arrived = lax.all_to_all(box, ROWS, split_axis=0, concat_axis=0, tiled=True)  12.5 us
    all_to_all x2, starting transfers between devices, along_z(): return lax.all_to_all(value, 'z', split_axis=0, concat_axis=0, tiled=True)  9.97 us
    all_to_all x1, starting transfers between devices, sum_over(): lax.all_to_all(copies, axes, split_axis=0, concat_axis=0, tiled=True)  9.56 us
    pallas_call x1, Pallas kernels, apply(): pl.pallas_call(functools.partial(apply_kernel, rows_dev), out_shape=jax.S...  9.3 us
    pallas_call x1, Pallas kernels, grad(): pl.pallas_call(functools.partial(grad_kernel, rows_dev), out_shape=(jax.S...  7.23 us
  transfers between devices with their start and end apart: 10, of which 5 were waited for; matrix products, arithmetic and copies ran while one was open for 5% of the time, Pallas kernels for 3%

profile of v5, /device:TPU:1, one launch (start us, length us, event | category | flops | bytes accessed | tf_op | source)
XLA Modules:
  0.0 146.8 jit_solution(867322755788176710)
XLA Ops:
  0.6 7.2 %grad.1 = (bf16[24,176,128]{2,1,0:T(8,128)(2,1)}, bf16[24,176,128]{2,1,0:T(8,128)(2,1)}) custom-call(s32[1]{0:T(128)} %bitcast.me_ref, bf16[512,128]{1,0:T(8,128)(2,1)} %cot_ref.1, bf16[512,8192]{1,0:T(8,128)(2,1)} %tokens_hbm.3), custom_call_target="tpu_custom_call" | custom-call | tf_op jit(solution)/shard_map/grad/pallas_call | solution.py:178
  7.9 12.5 %collective-permute-start.3 = (bf16[24,176,128]{2,1,0:T(8,128)(2,1)}, bf16[24,176,128]{2,1,0:T(8,128)(2,1)S(1)}, u32[]{:S(2)}, u32[]{:S(2)}) collective-permute-start(bf16[24,176,128]{2,1,0:T(8,128)(2,1)} %get-tuple-element.12), channel_id=1, source_target_pairs={{0,16},{16,0},{32,48},{48,32},{64,80},{80,64},{96,112},{112,96},{1... | collective-permute-start | bytes 3244040 | tf_op jit(solution)/shard_map/ppermute | solution.py:36
  20.4 2.2 %route.1 = bf16[48,32,128]{2,1,0:T(8,128)(2,1)} custom-call(s32[1,171]{1,0:T(1,128)} %bitcast.2, f32[171,128]{1,0:T(8,128)} %master_ref.1, f32[171,128]{1,0:T(8,128)} %first_ref.1, f32[171,128]{1,0:T(8,128)} %second_ref.1), custom_call_target="tpu_custom_call" | custom-call | tf_op jit(solution)/shard_map/route/pallas_call | solution.py:79
  22.6 6.0 %all-to-all-start = ((bf16[48,32,128]{2,1,0:T(8,128)(2,1)}), bf16[48,32,128]{2,1,0:T(8,128)(2,1)S(1)}, u32[]{:S(2)}, u32[]{:S(2)}) async-start(bf16[48,32,128]{2,1,0:T(8,128)(2,1)} %route.1), calls=%async_computation | async-start | bytes 786432 | tf_op jit(solution)/shard_map/all_to_all | solution.py:275
  28.8 4.5 %collective-permute-start.4 = (bf16[12,176,128]{2,1,0:T(8,128)(2,1)S(1)}, bf16[12,176,128]{2,1,0:T(8,128)(2,1)}, u32[]{:S(2)}, u32[]{:S(2)}) collective-permute-start(bf16[12,176,128]{2,1,0:T(8,128)(2,1)S(1)} %add_convert_fusion), channel_id=1, source_target_pairs={{0,32},{16,112},{32,0},{48,80},{64,96},{80,48},{96,64},{112,16},{1... | collective-permute-start | bytes 1622024 | tf_op jit(solution)/shard_map/ppermute | solution.py:36
  33.3 12.5 %all-to-all-done.box_ref = bf16[48,32,128]{2,1,0:T(8,128)(2,1)S(1)} async-done(((bf16[48,32,128]{2,1,0:T(8,128)(2,1)}), bf16[48,32,128]{2,1,0:T(8,128)(2,1)S(1)}, u32[]{:S(2)}, u32[]{:S(2)}) %all-to-all-start) | async-done | bytes 393248 | tf_op jit(solution)/shard_map/all_to_all | solution.py:275
  45.8 0.7 copy-done.1
  46.6 2.1 %place.1 = (bf16[6,176,128]{2,1,0:T(8,128)(2,1)}, f32[176,128]{1,0:T(8,128)}, f32[176,128]{1,0:T(8,128)}) custom-call(bf16[48,32,128]{2,1,0:T(8,128)(2,1)} %copy-done.1), custom_call_target="tpu_custom_call" | custom-call | tf_op jit(solution)/shard_map/place/pallas_call | solution.py:107
  48.7 6.5 %all-to-all-start.1 = ((bf16[6,176,128]{2,1,0:T(8,128)(2,1)}), bf16[6,176,128]{2,1,0:T(8,128)(2,1)S(1)}, u32[]{:S(2)}, u32[]{:S(2)}) async-start(bf16[6,176,128]{2,1,0:T(8,128)(2,1)} %get-tuple-element.9), calls=%async_computation.1 | async-start | bytes 540672 | tf_op jit(solution)/shard_map/all_to_all | solution.py:40
  55.2 1.1 add_convert_fusion.2
  56.3 1.9 %collective-permute-start.5 = (bf16[6,176,128]{2,1,0:T(8,128)(2,1)S(1)}, bf16[6,176,128]{2,1,0:T(8,128)(2,1)S(1)}, u32[]{:S(2)}, u32[]{:S(2)}) collective-permute-start(bf16[6,176,128]{2,1,0:T(8,128)(2,1)S(1)} %add_convert_fusion.2), channel_id=1, source_target_pairs={{0,96},{16,48},{32,64},{48,16},{64,32},{80,112},{96,0},{112,80},{1... | collective-permute-start | bytes 811016 | tf_op jit(solution)/shard_map/ppermute | solution.py:36
  58.2 10.3 %all-to-all-done.1 = bf16[6,176,128]{2,1,0:T(8,128)(2,1)S(1)} async-done(((bf16[6,176,128]{2,1,0:T(8,128)(2,1)}), bf16[6,176,128]{2,1,0:T(8,128)(2,1)S(1)}, u32[]{:S(2)}, u32[]{:S(2)}) %all-to-all-start.1) | async-done | bytes 270368 | tf_op jit(solution)/shard_map/all_to_all | solution.py:40
  68.4 2.2 %collective-permute-start = (bf16[6,176,128]{2,1,0:T(8,128)(2,1)S(1)}, bf16[6,176,128]{2,1,0:T(8,128)(2,1)S(1)}, u32[]{:S(2)}, u32[]{:S(2)}) collective-permute-start(bf16[6,176,128]{2,1,0:T(8,128)(2,1)S(1)} %all-to-all-done.1), channel_id=1, source_target_pairs={{0,32},{16,112},{32,0},{48,80},{64,96},{80,48},{96,64},{112,16},{1... | collective-permute-start | bytes 811016 | tf_op jit(solution)/shard_map/ppermute | solution.py:36
  70.7 1.8 %add_convert_fusion.1 = bf16[6,176,128]{2,1,0:T(8,128)(2,1)} fusion(bf16[6,176,128]{2,1,0:T(8,128)(2,1)S(1)} %collective-permute-done.5, bf16[24,176,128]{2,1,0:T(8,128)(2,1)S(1)} %collective-permute-done.3, bf16[12,176,128]{2,1,0:T(8,128)(2,1)} %collective-permute-done.4, bf16[24,176,128]{2,1,0:T(8,128)(2,1)S(1)} %copy-done.2), kind=kLoop, calls=%fused_computation.3 | loop fusion | flops 1081344 | bytes 1351680 | tf_op jit(solution)/shard_map/convert_element_type | solution.py:287
  72.5 3.4 %all-to-all-start.2 = ((bf16[6,176,128]{2,1,0:T(8,128)(2,1)}), bf16[6,176,128]{2,1,0:T(8,128)(2,1)S(1)}, u32[]{:S(2)}, u32[]{:S(2)}) async-start(bf16[6,176,128]{2,1,0:T(8,128)(2,1)} %add_convert_fusion.1), calls=%async_computation.2 | async-start | bytes 540672 | tf_op jit(solution)/shard_map/all_to_all | solution.py:40
  75.9 0.9 collective-permute-done
  76.9 1.9 %collective-permute-start.1 = (bf16[12,176,128]{2,1,0:T(8,128)(2,1)S(1)}, bf16[12,176,128]{2,1,0:T(8,128)(2,1)S(1)}, u32[]{:S(2)}, u32[]{:S(2)}) collective-permute-start(bf16[12,176,128]{2,1,0:T(8,128)(2,1)S(1)} %pad_maximum_fusion), channel_id=1, source_target_pairs={{0,96},{16,48},{32,64},{48,16},{64,32},{80,112},{96,0},{112,80},{1... | collective-permute-start | bytes 1622024 | tf_op jit(solution)/shard_map/ppermute | solution.py:36
  78.9 10.3 %all-to-all-done.2 = bf16[6,176,128]{2,1,0:T(8,128)(2,1)S(1)} async-done(((bf16[6,176,128]{2,1,0:T(8,128)(2,1)}), bf16[6,176,128]{2,1,0:T(8,128)(2,1)S(1)}, u32[]{:S(2)}, u32[]{:S(2)}) %all-to-all-start.2) | async-done | bytes 270368 | tf_op jit(solution)/shard_map/all_to_all | solution.py:40
  89.9 1.2 broadcast_in_dim.6
  91.1 9.6 %all-to-all-start.3 = ((f32[12,8,128]{2,1,0:T(8,128)}), f32[12,8,128]{2,1,0:T(8,128)S(1)}, u32[]{:S(2)}, u32[]{:S(2)}) async-start(f32[12,8,128]{2,1,0:T(8,128)} %broadcast_in_dim.6), calls=%async_computation.3 | async-start | bytes 98304 | tf_op jit(solution)/shard_map/all_to_all | solution.py:45
  100.8 3.9 %collective-permute-start.2 = (bf16[24,176,128]{2,1,0:T(8,128)(2,1)S(1)}, bf16[24,176,128]{2,1,0:T(8,128)(2,1)}, u32[]{:S(2)}, u32[]{:S(2)}) collective-permute-start(bf16[24,176,128]{2,1,0:T(8,128)(2,1)S(1)} %constant_dynamic-update-slice_fusion.mine_ref), channel_id=1, source_target_pairs={{0,16},{16,0},{32,48},{48,32},{64,80},{80,64},{96,112},{112,96},{1... | collective-permute-start | bytes 3244040 | tf_op jit(solution)/shard_map/ppermute | solution.py:36
  104.7 5.1 %all-to-all-done.3 = f32[12,8,128]{2,1,0:T(8,128)S(1)} async-done(((f32[12,8,128]{2,1,0:T(8,128)}), f32[12,8,128]{2,1,0:T(8,128)S(1)}, u32[]{:S(2)}, u32[]{:S(2)}) %all-to-all-start.3) | async-done | bytes 49184 | tf_op jit(solution)/shard_map/all_to_all | solution.py:45
  111.1 24.3 %all_to_all.25 = f32[64,8,128]{2,1,0:T(8,128)S(1)} all-to-all(f32[64,8,128]{2,1,0:T(8,128)S(1)} %broadcast_in_dim.7), channel_id=1, replica_groups=mesh['z'=6,'x'=4,'core'=2,'far'=2,'y'=8] {'x','core','y'}, dimensions={0} | all-to-all | bytes 524288 | tf_op jit(solution)/shard_map/all_to_all | solution.py:45
  137.5 9.3 %apply.1 = bf16[512,128]{1,0:T(8,128)(2,1)} custom-call(s32[1]{0:T(128)} %bitcast.me_ref, bf16[24,176,128]{2,1,0:T(8,128)(2,1)} %copy-done, bf16[24,176,128]{2,1,0:T(8,128)(2,1)} %collective-permute-done.2.other_hbm, bf16[512,8192]{1,0:T(8,128)(2,1)} %tokens_hbm.3), custom_call_target="tpu_custom_call" | custom-call | tf_op jit(solution)/shard_map/apply/pallas_call | solution.py:252
  (25 shorter events, 3.7 us)
Async XLA Ops:
  7.9 20.8 %copy-start.2 = (bf16[24,176,128]{2,1,0:T(8,128)(2,1)S(1)}, bf16[24,176,128]{2,1,0:T(8,128)(2,1)}, u32[]{:S(2)}) copy-start(bf16[24,176,128]{2,1,0:T(8,128)(2,1)} %get-tuple-element.11) | copy-start | bytes 3244036
  7.9 20.8 %collective-permute-start.3 = (bf16[24,176,128]{2,1,0:T(8,128)(2,1)}, bf16[24,176,128]{2,1,0:T(8,128)(2,1)S(1)}, u32[]{:S(2)}, u32[]{:S(2)}) collective-permute-start(bf16[24,176,128]{2,1,0:T(8,128)(2,1)} %get-tuple-element.12), channel_id=1, source_target_pairs={{0,16},{16,0},{32,48},{48,32},{64,80},{80,64},{96,112},{112,96},{1... | collective-permute-start | bytes 3244040 | tf_op jit(solution)/shard_map/ppermute | solution.py:36
  22.6 23.2 %all-to-all-start = ((bf16[48,32,128]{2,1,0:T(8,128)(2,1)}), bf16[48,32,128]{2,1,0:T(8,128)(2,1)S(1)}, u32[]{:S(2)}, u32[]{:S(2)}) async-start(bf16[48,32,128]{2,1,0:T(8,128)(2,1)} %route.1), calls=%async_computation | async-start | bytes 786432 | tf_op jit(solution)/shard_map/all_to_all | solution.py:275
  28.8 26.4 %collective-permute-start.4 = (bf16[12,176,128]{2,1,0:T(8,128)(2,1)S(1)}, bf16[12,176,128]{2,1,0:T(8,128)(2,1)}, u32[]{:S(2)}, u32[]{:S(2)}) collective-permute-start(bf16[12,176,128]{2,1,0:T(8,128)(2,1)S(1)} %add_convert_fusion), channel_id=1, source_target_pairs={{0,32},{16,112},{32,0},{48,80},{64,96},{80,48},{96,64},{112,16},{1... | collective-permute-start | bytes 1622024 | tf_op jit(solution)/shard_map/ppermute | solution.py:36
  45.8 0.7 copy-start.1
  48.7 19.8 %all-to-all-start.1 = ((bf16[6,176,128]{2,1,0:T(8,128)(2,1)}), bf16[6,176,128]{2,1,0:T(8,128)(2,1)S(1)}, u32[]{:S(2)}, u32[]{:S(2)}) async-start(bf16[6,176,128]{2,1,0:T(8,128)(2,1)} %get-tuple-element.9), calls=%async_computation.1 | async-start | bytes 540672 | tf_op jit(solution)/shard_map/all_to_all | solution.py:40
  56.3 14.4 %collective-permute-start.5 = (bf16[6,176,128]{2,1,0:T(8,128)(2,1)S(1)}, bf16[6,176,128]{2,1,0:T(8,128)(2,1)S(1)}, u32[]{:S(2)}, u32[]{:S(2)}) collective-permute-start(bf16[6,176,128]{2,1,0:T(8,128)(2,1)S(1)} %add_convert_fusion.2), channel_id=1, source_target_pairs={{0,96},{16,48},{32,64},{48,16},{64,32},{80,112},{96,0},{112,80},{1... | collective-permute-start | bytes 811016 | tf_op jit(solution)/shard_map/ppermute | solution.py:36
  68.4 8.4 %collective-permute-start = (bf16[6,176,128]{2,1,0:T(8,128)(2,1)S(1)}, bf16[6,176,128]{2,1,0:T(8,128)(2,1)S(1)}, u32[]{:S(2)}, u32[]{:S(2)}) collective-permute-start(bf16[6,176,128]{2,1,0:T(8,128)(2,1)S(1)} %all-to-all-done.1), channel_id=1, source_target_pairs={{0,32},{16,112},{32,0},{48,80},{64,96},{80,48},{96,64},{112,16},{1... | collective-permute-start | bytes 811016 | tf_op jit(solution)/shard_map/ppermute | solution.py:36
  72.5 16.7 %all-to-all-start.2 = ((bf16[6,176,128]{2,1,0:T(8,128)(2,1)}), bf16[6,176,128]{2,1,0:T(8,128)(2,1)S(1)}, u32[]{:S(2)}, u32[]{:S(2)}) async-start(bf16[6,176,128]{2,1,0:T(8,128)(2,1)} %add_convert_fusion.1), calls=%async_computation.2 | async-start | bytes 540672 | tf_op jit(solution)/shard_map/all_to_all | solution.py:40
  76.9 23.8 %collective-permute-start.1 = (bf16[12,176,128]{2,1,0:T(8,128)(2,1)S(1)}, bf16[12,176,128]{2,1,0:T(8,128)(2,1)S(1)}, u32[]{:S(2)}, u32[]{:S(2)}) collective-permute-start(bf16[12,176,128]{2,1,0:T(8,128)(2,1)S(1)} %pad_maximum_fusion), channel_id=1, source_target_pairs={{0,96},{16,48},{32,64},{48,16},{64,32},{80,112},{96,0},{112,80},{1... | collective-permute-start | bytes 1622024 | tf_op jit(solution)/shard_map/ppermute | solution.py:36
  89.2 47.6 %copy-start.3 = (f32[176,128]{1,0:T(8,128)S(1)}, f32[176,128]{1,0:T(8,128)}, u32[]{:S(2)}) copy-start(f32[176,128]{1,0:T(8,128)} %get-tuple-element.10) | copy-start | bytes 270340
  89.2 47.6 %copy-start.4 = (f32[176,128]{1,0:T(8,128)S(1)}, f32[176,128]{1,0:T(8,128)}, u32[]{:S(2)}) copy-start(f32[176,128]{1,0:T(8,128)} %get-tuple-element.15) | copy-start | bytes 270340
  91.1 18.7 %all-to-all-start.3 = ((f32[12,8,128]{2,1,0:T(8,128)}), f32[12,8,128]{2,1,0:T(8,128)S(1)}, u32[]{:S(2)}, u32[]{:S(2)}) async-start(f32[12,8,128]{2,1,0:T(8,128)} %broadcast_in_dim.6), calls=%async_computation.3 | async-start | bytes 98304 | tf_op jit(solution)/shard_map/all_to_all | solution.py:45
  100.8 36.8 %copy-start = (bf16[24,176,128]{2,1,0:T(8,128)(2,1)}, bf16[24,176,128]{2,1,0:T(8,128)(2,1)S(1)}, u32[]{:S(2)}) copy-start(bf16[24,176,128]{2,1,0:T(8,128)(2,1)S(1)} %constant_dynamic-update-slice_fusion.mine_ref) | copy-start | bytes 3244036
  100.8 36.8 %collective-permute-start.2 = (bf16[24,176,128]{2,1,0:T(8,128)(2,1)S(1)}, bf16[24,176,128]{2,1,0:T(8,128)(2,1)}, u32[]{:S(2)}, u32[]{:S(2)}) collective-permute-start(bf16[24,176,128]{2,1,0:T(8,128)(2,1)S(1)} %constant_dynamic-update-slice_fusion.mine_ref), channel_id=1, source_target_pairs={{0,16},{16,0},{32,48},{48,32},{64,80},{80,64},{96,112},{112,96},{1... | collective-permute-start | bytes 3244040 | tf_op jit(solution)/shard_map/ppermute | solution.py:36

commit v6 on v5

--- a/solution.py
+++ b/solution.py
@@ -40,10 +40,10 @@
     return lax.all_to_all(value, "z", split_axis=0, concat_axis=0, tiled=True)
 
 
-def sum_over(value, axes):
-    copies = jnp.broadcast_to(value, (lax.axis_size(axes), 8, 128))
+def sum_over(lanes, axes):
+    copies = jnp.broadcast_to(lanes, (lax.axis_size(axes), 8, 128))
     parts = lax.all_to_all(copies, axes, split_axis=0, concat_axis=0, tiled=True)
-    return jnp.sum(parts[:, 0, 0])
+    return jnp.sum(parts, axis=0)
 
 
 def iota(shape, axis):
@@ -294,12 +294,12 @@
     mine = jnp.concatenate([pair, rest], axis=0)
     other = shift(mine, dc=1)
 
-    squares = jnp.sum(gradient * gradient)
-    squares = sum_over(squares, ("z", "far"))
-    squares = sum_over(squares, ("x", "core", "y"))
+    squares = jnp.sum(gradient * gradient, axis=0)
+    squares = sum_over(squares, ("z", "core", "far"))
+    squares = sum_over(squares, ("x", "y"))
     keys_values = apply(me, mine, other, tokens, rows_dev)
 
-    factor = clip_norm / (jnp.sqrt(squares) + 1e-06)
+    factor = clip_norm / (jnp.sqrt(jnp.sum(squares) / 8.0) + 1e-06)
     clipped = gradient * factor
     moment_one = beta_one * first[:rows_dev] + (1.0 - beta_one) * clipped
     moment_two = beta_two * second[:rows_dev] + (1.0 - beta_two) * clipped * clipped

time: 148 us -> 143 us (0.966)
  blocking collectives: 24.3 us -> 42 us
  waiting for transfers between devices: 39.1 us -> 23.1 us
  starting transfers between devices: 52.6 us -> 44.8 us
    all_to_all x1 -> x2, blocking collectives: 24.3 us -> 42 us  [sum_over(): lax.all_to_all(copies, axes, split_axis=0, concat_axis=0, tiled=True)]
    all_to_all x2, waiting for transfers between devices: 20.5 us -> 9.32 us  [along_z(): return lax.all_to_all(value, 'z', split_axis=0, concat_axis=0, tiled=True)]
    all_to_all x1, starting transfers between devices: 6.04 us -> 16.4 us  [per_device(): arrived = lax.all_to_all(box, ROWS, split_axis=0, concat_axis=0, tiled=True)]
    all_to_all x1 -> x0, starting transfers between devices: 9.56 us -> none  [sum_over(): lax.all_to_all(copies, axes, split_axis=0, concat_axis=0, tiled=True)]
    ppermute x6, starting transfers between devices: 27 us -> 17.8 us  [shift(): return lax.ppermute(value, ROWS, pairs)]
    ppermute x6, waiting for transfers between devices: 0.95 us -> 6.13 us  [shift(): return lax.ppermute(value, ROWS, pairs)]
    all_to_all x1 -> x0, waiting for transfers between devices: 5.11 us -> none  [sum_over(): lax.all_to_all(copies, axes, split_axis=0, concat_axis=0, tiled=True)]
    all_to_all x1, waiting for transfers between devices: 12.5 us -> 7.67 us  [per_device(): arrived = lax.all_to_all(box, ROWS, split_axis=0, concat_axis=0, tiled=True)]
  transfers between devices with their start and end apart: 10 -> 9, of which waited for: 5 -> 6; matrix products, arithmetic and copies ran while one was open for 5% -> 6% of each run, Pallas kernels for 3% -> 7%
where the time goes in v6:
time: 143 us; the launch traced here: 141 us
  starting transfers between devices  44.8 us (31%)
  blocking collectives  42 us (29%)
  waiting for transfers between devices  23.1 us (16%)
  Pallas kernels  20.8 us (15%)
  other arithmetic  7.21 us (5%)
  local copies, waits for them, and re-layouts  1.97 us (1%)
  between operations  1.56 us (1%)
    all_to_all x2, blocking collectives, sum_over(): lax.all_to_all(copies, axes, split_axis=0, concat_axis=0, tiled=True)  42 us
    ppermute x6, starting transfers between devices, shift(): return lax.ppermute(value, ROWS, pairs)  17.8 us
    all_to_all x1, starting transfers between devices, per_device(): arrived = lax.all_to_all(box, ROWS, split_axis=0, concat_axis=0, tiled=True)  16.4 us
    all_to_all x2, starting transfers between devices, along_z(): return lax.all_to_all(value, 'z', split_axis=0, concat_axis=0, tiled=True)  10.6 us
    all_to_all x2, waiting for transfers between devices, along_z(): return lax.all_to_all(value, 'z', split_axis=0, concat_axis=0, tiled=True)  9.32 us
    pallas_call x1, Pallas kernels, apply(): pl.pallas_call(functools.partial(apply_kernel, rows_dev), out_shape=jax.S...  9.29 us
    all_to_all x1, waiting for transfers between devices, per_device(): arrived = lax.all_to_all(box, ROWS, split_axis=0, concat_axis=0, tiled=True)  7.67 us
    pallas_call x1, Pallas kernels, grad(): pl.pallas_call(functools.partial(grad_kernel, rows_dev), out_shape=(jax.S...  7.23 us
  transfers between devices with their start and end apart: 9, of which 6 were waited for; matrix products, arithmetic and copies ran while one was open for 6% of the time, Pallas kernels for 7%

profile of v6, /device:TPU:1, one launch (start us, length us, event | category | flops | bytes accessed | tf_op | source)
XLA Modules:
  0.0 141.4 jit_solution(17569593716045150179)
XLA Ops:
  0.6 2.2 %route.1 = bf16[48,32,128]{2,1,0:T(8,128)(2,1)} custom-call(s32[1,171]{1,0:T(1,128)} %bitcast.2, f32[171,128]{1,0:T(8,128)} %master_ref.1, f32[171,128]{1,0:T(8,128)} %first_ref.1, f32[171,128]{1,0:T(8,128)} %second_ref.1), custom_call_target="tpu_custom_call" | custom-call | tf_op jit(solution)/shard_map/route/pallas_call | solution.py:79
  2.8 16.4 %all-to-all-start = ((bf16[48,32,128]{2,1,0:T(8,128)(2,1)}), bf16[48,32,128]{2,1,0:T(8,128)(2,1)S(1)}, u32[]{:S(2)}, u32[]{:S(2)}) async-start(bf16[48,32,128]{2,1,0:T(8,128)(2,1)} %route.1), calls=%async_computation | async-start | bytes 786432 | tf_op jit(solution)/shard_map/all_to_all | solution.py:275
  19.2 7.2 %grad.1 = (bf16[24,176,128]{2,1,0:T(8,128)(2,1)}, bf16[24,176,128]{2,1,0:T(8,128)(2,1)}) custom-call(s32[1]{0:T(128)} %bitcast.me_ref, bf16[512,128]{1,0:T(8,128)(2,1)} %cot_ref.1, bf16[512,8192]{1,0:T(8,128)(2,1)} %tokens_hbm.3), custom_call_target="tpu_custom_call" | custom-call | tf_op jit(solution)/shard_map/grad/pallas_call | solution.py:178
  26.5 2.3 %collective-permute-start.3 = (bf16[24,176,128]{2,1,0:T(8,128)(2,1)}, bf16[24,176,128]{2,1,0:T(8,128)(2,1)S(1)}, u32[]{:S(2)}, u32[]{:S(2)}) collective-permute-start(bf16[24,176,128]{2,1,0:T(8,128)(2,1)} %get-tuple-element.12), channel_id=1, source_target_pairs={{0,16},{16,0},{32,48},{48,32},{64,80},{80,64},{96,112},{112,96},{1... | collective-permute-start | bytes 3244040 | tf_op jit(solution)/shard_map/ppermute | solution.py:36
  28.7 7.7 %all-to-all-done.box_ref = bf16[48,32,128]{2,1,0:T(8,128)(2,1)S(1)} async-done(((bf16[48,32,128]{2,1,0:T(8,128)(2,1)}), bf16[48,32,128]{2,1,0:T(8,128)(2,1)S(1)}, u32[]{:S(2)}, u32[]{:S(2)}) %all-to-all-start) | async-done | bytes 393248 | tf_op jit(solution)/shard_map/all_to_all | solution.py:275
  37.2 2.1 %place.1 = (bf16[6,176,128]{2,1,0:T(8,128)(2,1)}, f32[176,128]{1,0:T(8,128)}, f32[176,128]{1,0:T(8,128)}) custom-call(bf16[48,32,128]{2,1,0:T(8,128)(2,1)} %copy-done.1), custom_call_target="tpu_custom_call" | custom-call | tf_op jit(solution)/shard_map/place/pallas_call | solution.py:107
  39.2 6.7 %all-to-all-start.1 = ((bf16[6,176,128]{2,1,0:T(8,128)(2,1)}), bf16[6,176,128]{2,1,0:T(8,128)(2,1)S(1)}, u32[]{:S(2)}, u32[]{:S(2)}) async-start(bf16[6,176,128]{2,1,0:T(8,128)(2,1)} %get-tuple-element.9), calls=%async_computation.1 | async-start | bytes 540672 | tf_op jit(solution)/shard_map/all_to_all | solution.py:40
  45.9 2.0 %add_convert_fusion = bf16[12,176,128]{2,1,0:T(8,128)(2,1)} fusion(bf16[24,176,128]{2,1,0:T(8,128)(2,1)S(1)} %collective-permute-done.3, bf16[24,176,128]{2,1,0:T(8,128)(2,1)} %get-tuple-element.11), kind=kLoop, calls=%fused_computation | loop fusion | flops 1081344 | bytes 1622016 | tf_op jit(solution)/shard_map/convert_element_type | solution.py:280
  47.9 2.2 %collective-permute-start.4 = (bf16[12,176,128]{2,1,0:T(8,128)(2,1)}, bf16[12,176,128]{2,1,0:T(8,128)(2,1)}, u32[]{:S(2)}, u32[]{:S(2)}) collective-permute-start(bf16[12,176,128]{2,1,0:T(8,128)(2,1)} %add_convert_fusion), channel_id=1, source_target_pairs={{0,32},{16,112},{32,0},{48,80},{64,96},{80,48},{96,64},{112,16},{1... | collective-permute-start | bytes 1622024 | tf_op jit(solution)/shard_map/ppermute | solution.py:36
  50.1 9.0 %all-to-all-done.1 = bf16[6,176,128]{2,1,0:T(8,128)(2,1)S(1)} async-done(((bf16[6,176,128]{2,1,0:T(8,128)(2,1)}), bf16[6,176,128]{2,1,0:T(8,128)(2,1)S(1)}, u32[]{:S(2)}, u32[]{:S(2)}) %all-to-all-start.1) | async-done | bytes 270368 | tf_op jit(solution)/shard_map/all_to_all | solution.py:40
  59.1 2.2 %collective-permute-start = (bf16[6,176,128]{2,1,0:T(8,128)(2,1)S(1)}, bf16[6,176,128]{2,1,0:T(8,128)(2,1)S(1)}, u32[]{:S(2)}, u32[]{:S(2)}) collective-permute-start(bf16[6,176,128]{2,1,0:T(8,128)(2,1)S(1)} %all-to-all-done.1), channel_id=1, source_target_pairs={{0,32},{16,112},{32,0},{48,80},{64,96},{80,48},{96,64},{112,16},{1... | collective-permute-start | bytes 811016 | tf_op jit(solution)/shard_map/ppermute | solution.py:36
  61.4 1.1 add_convert_fusion.2
  62.5 1.9 %collective-permute-start.5 = (bf16[6,176,128]{2,1,0:T(8,128)(2,1)S(1)}, bf16[6,176,128]{2,1,0:T(8,128)(2,1)S(1)}, u32[]{:S(2)}, u32[]{:S(2)}) collective-permute-start(bf16[6,176,128]{2,1,0:T(8,128)(2,1)S(1)} %add_convert_fusion.2), channel_id=1, source_target_pairs={{0,96},{16,48},{32,64},{48,16},{64,32},{80,112},{96,0},{112,80},{1... | collective-permute-start | bytes 811016 | tf_op jit(solution)/shard_map/ppermute | solution.py:36
  64.4 3.2 %collective-permute-done = bf16[6,176,128]{2,1,0:T(8,128)(2,1)S(1)} collective-permute-done((bf16[6,176,128]{2,1,0:T(8,128)(2,1)S(1)}, bf16[6,176,128]{2,1,0:T(8,128)(2,1)S(1)}, u32[]{:S(2)}, u32[]{:S(2)}) %collective-permute-start) | collective-permute-done | bytes 270368 | tf_op jit(solution)/shard_map/ppermute | solution.py:36
  68.4 1.9 %collective-permute-start.1 = (bf16[12,176,128]{2,1,0:T(8,128)(2,1)}, bf16[12,176,128]{2,1,0:T(8,128)(2,1)}, u32[]{:S(2)}, u32[]{:S(2)}) collective-permute-start(bf16[12,176,128]{2,1,0:T(8,128)(2,1)} %pad_maximum_fusion), channel_id=1, source_target_pairs={{0,96},{16,48},{32,64},{48,16},{64,32},{80,112},{96,0},{112,80},{1... | collective-permute-start | bytes 1622024 | tf_op jit(solution)/shard_map/ppermute | solution.py:36
  70.3 1.4 collective-permute-done.5
  71.7 1.8 %add_convert_fusion.1 = bf16[6,176,128]{2,1,0:T(8,128)(2,1)} fusion(bf16[6,176,128]{2,1,0:T(8,128)(2,1)S(1)} %collective-permute-done.5, bf16[24,176,128]{2,1,0:T(8,128)(2,1)S(1)} %collective-permute-done.3, bf16[12,176,128]{2,1,0:T(8,128)(2,1)} %collective-permute-done.4, bf16[24,176,128]{2,1,0:T(8,128)(2,1)S(1)} %copy-done.2), kind=kLoop, calls=%fused_computation.3 | loop fusion | flops 1081344 | bytes 1351680 | tf_op jit(solution)/shard_map/convert_element_type | solution.py:287
  73.5 3.9 %all-to-all-start.2 = ((bf16[6,176,128]{2,1,0:T(8,128)(2,1)}), bf16[6,176,128]{2,1,0:T(8,128)(2,1)S(1)}, u32[]{:S(2)}, u32[]{:S(2)}) async-start(bf16[6,176,128]{2,1,0:T(8,128)(2,1)} %add_convert_fusion.1), calls=%async_computation.2 | async-start | bytes 540672 | tf_op jit(solution)/shard_map/all_to_all | solution.py:40
  77.5 1.6 %collective-permute-done.1 = bf16[12,176,128]{2,1,0:T(8,128)(2,1)} collective-permute-done((bf16[12,176,128]{2,1,0:T(8,128)(2,1)}, bf16[12,176,128]{2,1,0:T(8,128)(2,1)}, u32[]{:S(2)}, u32[]{:S(2)}) %collective-permute-start.1) | collective-permute-done | bytes 540704 | tf_op jit(solution)/shard_map/ppermute | solution.py:36
  79.1 1.1 constant_dynamic-update-slice_fusion.mine_ref
  80.2 7.3 %collective-permute-start.2 = (bf16[24,176,128]{2,1,0:T(8,128)(2,1)S(1)}, bf16[24,176,128]{2,1,0:T(8,128)(2,1)}, u32[]{:S(2)}, u32[]{:S(2)}) collective-permute-start(bf16[24,176,128]{2,1,0:T(8,128)(2,1)S(1)} %constant_dynamic-update-slice_fusion.mine_ref), channel_id=1, source_target_pairs={{0,16},{16,0},{32,48},{48,32},{64,80},{80,64},{96,112},{112,96},{1... | collective-permute-start | bytes 3244040 | tf_op jit(solution)/shard_map/ppermute | solution.py:36
  87.9 25.5 %all_to_all.25 = f32[24,8,128]{2,1,0:T(8,128)S(1)} all-to-all(f32[24,8,128]{2,1,0:T(8,128)S(1)} %broadcast_in_dim.6), channel_id=1, replica_groups=mesh['z'=6,'x'=4,'core'=2,'far'=2,'y'=8] {'z','core','far'}, dimensions={0} | all-to-all | bytes 196608 | tf_op jit(solution)/shard_map/all_to_all | solution.py:45
  113.4 16.5 %all_to_all.26 = f32[32,8,128]{2,1,0:T(8,128)S(1)} all-to-all(f32[32,8,128]{2,1,0:T(8,128)S(1)} %broadcast_in_dim.7), channel_id=1, replica_groups=mesh['z'=6,'x'=4,'core'=2,'far'=2,'y'=8] {'x','y'}, dimensions={0} | all-to-all | bytes 262144 | tf_op jit(solution)/shard_map/all_to_all | solution.py:45
  132.1 9.3 %apply.1 = bf16[512,128]{1,0:T(8,128)(2,1)} custom-call(s32[1]{0:T(128)} %bitcast.me_ref, bf16[24,176,128]{2,1,0:T(8,128)(2,1)} %copy-done, bf16[24,176,128]{2,1,0:T(8,128)(2,1)} %collective-permute-done.2.other_hbm, bf16[512,8192]{1,0:T(8,128)(2,1)} %tokens_hbm.3), custom_call_target="tpu_custom_call" | custom-call | tf_op jit(solution)/shard_map/apply/pallas_call | solution.py:252
  (24 shorter events, 3.5 us)
Async XLA Ops:
  2.8 33.6 %all-to-all-start = ((bf16[48,32,128]{2,1,0:T(8,128)(2,1)}), bf16[48,32,128]{2,1,0:T(8,128)(2,1)S(1)}, u32[]{:S(2)}, u32[]{:S(2)}) async-start(bf16[48,32,128]{2,1,0:T(8,128)(2,1)} %route.1), calls=%async_computation | async-start | bytes 786432 | tf_op jit(solution)/shard_map/all_to_all | solution.py:275
  26.5 19.4 %collective-permute-start.3 = (bf16[24,176,128]{2,1,0:T(8,128)(2,1)}, bf16[24,176,128]{2,1,0:T(8,128)(2,1)S(1)}, u32[]{:S(2)}, u32[]{:S(2)}) collective-permute-start(bf16[24,176,128]{2,1,0:T(8,128)(2,1)} %get-tuple-element.12), channel_id=1, source_target_pairs={{0,16},{16,0},{32,48},{48,32},{64,80},{80,64},{96,112},{112,96},{1... | collective-permute-start | bytes 3244040 | tf_op jit(solution)/shard_map/ppermute | solution.py:36
  36.4 0.8 copy-start.1
  39.2 22.2 %copy-start.2 = (bf16[24,176,128]{2,1,0:T(8,128)(2,1)S(1)}, bf16[24,176,128]{2,1,0:T(8,128)(2,1)}, u32[]{:S(2)}) copy-start(bf16[24,176,128]{2,1,0:T(8,128)(2,1)} %get-tuple-element.11) | copy-start | bytes 3244036
  39.2 19.9 %all-to-all-start.1 = ((bf16[6,176,128]{2,1,0:T(8,128)(2,1)}), bf16[6,176,128]{2,1,0:T(8,128)(2,1)S(1)}, u32[]{:S(2)}, u32[]{:S(2)}) async-start(bf16[6,176,128]{2,1,0:T(8,128)(2,1)} %get-tuple-element.9), calls=%async_computation.1 | async-start | bytes 540672 | tf_op jit(solution)/shard_map/all_to_all | solution.py:40
  47.9 13.5 %collective-permute-start.4 = (bf16[12,176,128]{2,1,0:T(8,128)(2,1)}, bf16[12,176,128]{2,1,0:T(8,128)(2,1)}, u32[]{:S(2)}, u32[]{:S(2)}) collective-permute-start(bf16[12,176,128]{2,1,0:T(8,128)(2,1)} %add_convert_fusion), channel_id=1, source_target_pairs={{0,32},{16,112},{32,0},{48,80},{64,96},{80,48},{96,64},{112,16},{1... | collective-permute-start | bytes 1622024 | tf_op jit(solution)/shard_map/ppermute | solution.py:36
  59.1 8.4 %collective-permute-start = (bf16[6,176,128]{2,1,0:T(8,128)(2,1)S(1)}, bf16[6,176,128]{2,1,0:T(8,128)(2,1)S(1)}, u32[]{:S(2)}, u32[]{:S(2)}) collective-permute-start(bf16[6,176,128]{2,1,0:T(8,128)(2,1)S(1)} %all-to-all-done.1), channel_id=1, source_target_pairs={{0,32},{16,112},{32,0},{48,80},{64,96},{80,48},{96,64},{112,16},{1... | collective-permute-start | bytes 811016 | tf_op jit(solution)/shard_map/ppermute | solution.py:36
  62.5 9.2 %collective-permute-start.5 = (bf16[6,176,128]{2,1,0:T(8,128)(2,1)S(1)}, bf16[6,176,128]{2,1,0:T(8,128)(2,1)S(1)}, u32[]{:S(2)}, u32[]{:S(2)}) collective-permute-start(bf16[6,176,128]{2,1,0:T(8,128)(2,1)S(1)} %add_convert_fusion.2), channel_id=1, source_target_pairs={{0,96},{16,48},{32,64},{48,16},{64,32},{80,112},{96,0},{112,80},{1... | collective-permute-start | bytes 811016 | tf_op jit(solution)/shard_map/ppermute | solution.py:36
  68.4 10.7 %collective-permute-start.1 = (bf16[12,176,128]{2,1,0:T(8,128)(2,1)}, bf16[12,176,128]{2,1,0:T(8,128)(2,1)}, u32[]{:S(2)}, u32[]{:S(2)}) collective-permute-start(bf16[12,176,128]{2,1,0:T(8,128)(2,1)} %pad_maximum_fusion), channel_id=1, source_target_pairs={{0,96},{16,48},{32,64},{48,16},{64,32},{80,112},{96,0},{112,80},{1... | collective-permute-start | bytes 1622024 | tf_op jit(solution)/shard_map/ppermute | solution.py:36
  73.5 14.4 %all-to-all-start.2 = ((bf16[6,176,128]{2,1,0:T(8,128)(2,1)}), bf16[6,176,128]{2,1,0:T(8,128)(2,1)S(1)}, u32[]{:S(2)}, u32[]{:S(2)}) async-start(bf16[6,176,128]{2,1,0:T(8,128)(2,1)} %add_convert_fusion.1), calls=%async_computation.2 | async-start | bytes 540672 | tf_op jit(solution)/shard_map/all_to_all | solution.py:40
  77.5 53.9 %copy-start.3 = (f32[176,128]{1,0:T(8,128)S(1)}, f32[176,128]{1,0:T(8,128)}, u32[]{:S(2)}) copy-start(f32[176,128]{1,0:T(8,128)} %get-tuple-element.10) | copy-start | bytes 270340
  77.5 53.9 %copy-start.4 = (f32[176,128]{1,0:T(8,128)S(1)}, f32[176,128]{1,0:T(8,128)}, u32[]{:S(2)}) copy-start(f32[176,128]{1,0:T(8,128)} %get-tuple-element.15) | copy-start | bytes 270340
  80.2 51.9 %copy-start = (bf16[24,176,128]{2,1,0:T(8,128)(2,1)}, bf16[24,176,128]{2,1,0:T(8,128)(2,1)S(1)}, u32[]{:S(2)}) copy-start(bf16[24,176,128]{2,1,0:T(8,128)(2,1)S(1)} %constant_dynamic-update-slice_fusion.mine_ref) | copy-start | bytes 3244036
  80.2 51.9 %collective-permute-start.2 = (bf16[24,176,128]{2,1,0:T(8,128)(2,1)S(1)}, bf16[24,176,128]{2,1,0:T(8,128)(2,1)}, u32[]{:S(2)}, u32[]{:S(2)}) collective-permute-start(bf16[24,176,128]{2,1,0:T(8,128)(2,1)S(1)} %constant_dynamic-update-slice_fusion.mine_ref), channel_id=1, source_target_pairs={{0,16},{16,0},{32,48},{48,32},{64,80},{80,64},{96,112},{112,96},{1... | collective-permute-start | bytes 3244040 | tf_op jit(solution)/shard_map/ppermute | solution.py:36
